TPU v7x, 32 devices: a whole 2x2x4 slice. The times are simulated.
32 devices in a mesh: grp: 2 (over y), dep: 4 (over z), hgt: 2 (over x), wid: 2 (over core).
Axes of the slice: x: 2, y: 2, z: 4, core: 2. Of those that a mesh axis runs over, the one named last changes fastest.
Arguments:
- features: bfloat16 [64, 8, 16, 256], P('grp', 'wid', 'dep', 'hgt'), parts along dimension 0, may hold values from -6 to 6
- cotangent: bfloat16 [64, 8, 16, 256], P('grp', 'wid', 'dep', 'hgt'), parts along dimension 0, may hold values from -6 to 6
- w_stem: bfloat16 [3, 3, 3, 32, 32], replicated, may hold values from -0.21875 to 0.21875
- w_middle: bfloat16 [3, 3, 3, 32, 64], replicated, may hold values from -0.21875 to 0.21875
- w_bottom: bfloat16 [3, 3, 3, 64, 128], replicated, may hold values from -0.15625 to 0.15625
- w_rise: bfloat16 [3, 3, 3, 192, 64], replicated, may hold values from -0.078125 to 0.078125
- w_final: bfloat16 [3, 3, 3, 96, 32], replicated, may hold values from -0.125 to 0.125
Outputs:
- output: bfloat16 [64, 8, 16, 256], P('grp', 'wid', 'dep', 'hgt'), parts along dimension 0
- grad_stem: float32 [6, 3, 3, 32, 32], P('grp'), parts along dimension 0
- grad_middle: float32 [6, 3, 3, 32, 64], P('grp'), parts along dimension 0
- grad_bottom: float32 [6, 3, 3, 64, 128], P('grp'), parts along dimension 0
- grad_rise: float32 [6, 3, 3, 192, 64], P('grp'), parts along dimension 0
- grad_final: float32 [6, 3, 3, 96, 32], P('grp'), parts along dimension 0
- half_grad: float32 [64, 4, 8, 128], P('grp', 'wid', 'dep', 'hgt'), parts along dimension 0
There are 2 independent parts, one for each index of `grp`. A program takes and returns all parts, laid end to end along the dimension named above; an argument that names none is the same for every part. Nothing has to cross between parts.
All inputs are finite; a program needn't handle non-finite values.
Results may differ from a plain program's by a relative error of at most 0.012.
Values may be sent and summed in bfloat16 or wider, within the bound.
A program may use at most 128 MiB of HBM per device.

v0:
```python
import functools
import math

import jax
import jax.numpy as jnp
from jax import lax
from jax.experimental import pallas as pl
from jax.experimental.pallas import tpu as pltpu
from jax.sharding import PartitionSpec as P

BF, F32 = jnp.bfloat16, jnp.float32
SEGMENTS = ((3,), (2, 4), (1, 0))
AXES = ("grp", "dep", "hgt", "wid")


def mm(a, b):
    return lax.dot_general(a, b, (((1,), (0,)), ((), ())), preferred_element_type=F32)


def mm_nt(a, b):
    return lax.dot_general(a, b, (((1,), (1,)), ((), ())), preferred_element_type=F32)


def mm_split(a, b):
    high = a.astype(BF)
    low = (a - high.astype(F32)).astype(BF)
    return mm(high, b) + mm(low, b)


def silu(v):
    return v * jax.nn.sigmoid(v)


def slope(v):
    g = jax.nn.sigmoid(v)
    return g * (1.0 + v * (1.0 - g))


def pattern(lanes, test):
    row = lax.broadcasted_iota(jnp.int32, (lanes, lanes), 0)
    col = lax.broadcasted_iota(jnp.int32, (lanes, lanes), 1)
    return jnp.where(test(row, col), 1.0, 0.0)


class Halo:
    def __init__(self, index, rows, edges, own, span, sems):
        self.index, self.rows, self.edges, self.own = index, rows, edges, own
        self.w, self.d, self.h = span
        self.send, self.recv = sems

    def fill_edges(self):
        lanes = self.own.shape[1]
        lane = lax.broadcasted_iota(jnp.int32, self.own.shape, 1)
        tile = jnp.zeros(self.own.shape, F32)
        for a in range(self.w):
            for b in range(self.d):
                r = a * self.d + b
                row = self.rows[a + 1, b + 1].astype(F32)
                tile = jnp.where(lane == r, row[:, 0:1], tile)
                tile = jnp.where(lane == lanes // 2 + r, row[:, self.h - 1 : self.h], tile)
        self.own[...] = tile.astype(BF)

    def copies(self, build=True):
        place = {name: lax.axis_index(name) for name in AXES}
        size = {name: lax.axis_size(name) for name in AXES}

        def choices(name):
            i, n = place[name], size[name]
            if n == 1:
                return [(0, 0, True, True)]
            if n == 2:
                return [(0, 0, True, True), (1, 1 - 2 * i, True, True)]
            return [(0, 0, True, True), (1, 1, i < n - 1, i > 0), (2, -1, i > 0, i < n - 1)]

        def cells(step, code, count):
            if code == 0:
                return pl.ds(1, count), pl.ds(1, count)
            up = (1 + step) // 2
            return pl.ds(1 + (count - 1) * up, 1), pl.ds((count + 1) * (1 - up), 1)

        out = []
        for cw, sw, ow, iw in choices("wid"):
            for cd, sd, od, id_ in choices("dep"):
                for ch, sh, oh, ih in choices("hgt"):
                    if cw == 0 and cd == 0 and ch == 0:
                        continue
                    slot = self.index * 27 + (cw * 3 + cd) * 3 + ch
                    target = {"wid": place["wid"] + sw, "dep": place["dep"] + sd, "hgt": place["hgt"] + sh}
                    if not build:
                        out.append((target, [c for c in (ow, od, oh) if c is not True], [c for c in (iw, id_, ih) if c is not True]))
                        continue
                    if ch == 0:
                        from_w, to_w = cells(sw, cw, self.w)
                        from_d, to_d = cells(sd, cd, self.d)
                        source = self.rows.at[from_w, from_d]
                        dest = self.rows.at[to_w, to_d]
                    else:
                        source = self.own
                        dest = self.edges.at[(1 - sh) // 2, 1 - sw, 1 - sd]
                    copy = pltpu.make_async_remote_copy(
                        src_ref=source,
                        dst_ref=dest,
                        send_sem=self.send.at[slot],
                        recv_sem=self.recv.at[slot],
                        device_id=target,
                        device_id_type=pl.DeviceIdType.MESH,
                    )
                    out.append((copy, [c for c in (ow, od, oh) if c is not True], [c for c in (iw, id_, ih) if c is not True]))
        return out

    @staticmethod
    def guarded(conditions, action):
        if not conditions:
            action()
        else:
            pl.when(functools.reduce(jnp.logical_and, conditions))(action)

    def start(self):
        self.fill_edges()
        for copy, can_send, _ in self.copies():
            self.guarded(can_send, copy.start)

    def wait(self):
        for copy, _, can_take in self.copies():
            self.guarded(can_take, copy.wait_recv)

    def finish(self):
        for copy, can_send, _ in self.copies():
            self.guarded(can_send, copy.wait_send)

    def shifted(self, a, b, spread=None, fine=None):
        lanes = self.own.shape[1]
        h = self.h if spread is None else 2 * self.h
        row = self.rows[a, b]
        if spread is not None:
            row = mm(row, spread).astype(BF)
        dw = 0 if a == 0 else 2 if a == self.w + 1 else 1
        dd = 0 if b == 0 else 2 if b == self.d + 1 else 1
        r = (self.w - 1, a - 1, 0)[dw] * self.d + (self.d - 1, b - 1, 0)[dd]
        left = self.edges[0, dw, dd].astype(F32)[:, lanes // 2 + r : lanes // 2 + r + 1]
        right = self.edges[1, dw, dd].astype(F32)[:, r : r + 1]
        lane = lax.broadcasted_iota(jnp.int32, row.shape, 1)
        wide = row.astype(F32)
        before = jnp.where(lane == 0, left, pltpu.roll(wide, 1, 1))
        after = jnp.where(lane == h - 1, right, pltpu.roll(wide, lanes - 1, 1))
        if h < lanes:
            before = jnp.where(lane < h, before, 0.0)
            after = jnp.where(lane < h, after, 0.0)
        return before.astype(BF), row, after.astype(BF)


def at(name, position):
    return {n: position if n == name else lax.axis_index(n) for n in ("dep", "hgt", "wid")}


class Summed:
    order = ("wid", "hgt", "dep")

    def __init__(self, full, buffers, send, recv):
        self.total = buffers[0]
        self.levels = [(buffers[0], buffers[1], buffers[2]), buffers[3:6], buffers[6:9]]
        self.full, self.send, self.recv = full, send, recv
        self.stage, self.open, self.sent = 0, [], []

    def exchange(self, stage, name, pieces):
        i, n = lax.axis_index(name), lax.axis_size(name)
        self.open = []
        for k in range(1, n):
            source, dest = pieces(lax.rem(i + k, n), i)
            copy = pltpu.make_async_remote_copy(
                src_ref=source,
                dst_ref=dest,
                send_sem=self.send.at[stage, k],
                recv_sem=self.recv.at[stage, k],
                device_id=at(name, lax.rem(i + k, n)),
                device_id_type=pl.DeviceIdType.MESH,
            )
            copy.start()
            self.open.append(copy)
            self.sent.append(copy)

    def arrive(self):
        for copy in self.open:
            copy.wait_recv()
        self.open = []

    def step(self):
        stage = self.stage
        self.stage += 1
        if stage > 0:
            self.arrive()
        if 0 < stage <= 3:
            name = self.order[stage - 1]
            i, n = lax.axis_index(name), lax.axis_size(name)
            held, _, came = self.levels[stage - 1]
            m = held.shape[0] // n
            value = held[part(i, m)]
            for k in range(1, n):
                value = value + came[part(lax.rem(i + k, n), m)].astype(F32)
            if stage < 3:
                self.levels[stage][0][...] = value
            else:
                place = 0
                for axis in self.order:
                    place = place * lax.axis_size(axis) + lax.axis_index(axis)
                self.full[part(place, m)] = value.astype(BF)
        if stage < 3:
            held, wire, came = self.levels[stage]
            m = held.shape[0] // lax.axis_size(self.order[stage])
            wire[...] = held[...].astype(BF)
            self.exchange(stage, self.order[stage], lambda to, me: (wire.at[part(to, m)], came.at[part(me, m)]))
        elif stage < 6:
            depth = 6 - stage
            place, count = 0, 1
            for axis in self.order[:depth]:
                place = place * lax.axis_size(axis) + lax.axis_index(axis)
                count *= lax.axis_size(axis)
            m = self.full.shape[0] // count
            piece = self.full.at[part(place, m)]
            self.exchange(stage, self.order[depth - 1], lambda to, me: (piece, piece))

    def finish(self):
        while self.stage < 7:
            self.step()
        for copy in self.sent:
            copy.wait_send()


def part(i, m):
    return pl.ds(pl.multiple_of(i * m, 16), m)


def step_kernel(cfg, *refs):
    (f0, f1, f2, w, d, h) = cfg
    (feat, cot, raw_stem, raw_mid, raw_bot, w_rise, w_fin, b_rise, b_fin) = refs[:9]
    (output, full0, full1, full2, half_out) = refs[9:14]
    names = ("feat", "cot", "stem", "half", "mid", "quarter", "deep", "ra", "rg", "dg", "mg")
    refs = refs[14:]
    spans = {0: (w, d, h), 1: (w // 2, d // 2, h // 2), 2: (w // 4, d // 4, h // 4)}
    levels = dict(feat=0, cot=0, stem=0, half=1, mid=1, quarter=2, deep=2, ra=1, rg=1, dg=2, mg=1)
    send, recv = refs[0], refs[1]
    halo = {}
    for i, name in enumerate(names):
        rows, edges, own = refs[2 + 3 * i : 5 + 3 * i]
        halo[name] = Halo(i, rows, edges, own, spans[levels[name]], (send, recv))
    rest = refs[2 + 3 * len(names) :]
    (s_feat, s_cot, s_half, s_quarter, s_rise, s_fin, s_rg, s_dg, s_mg) = rest[:9]
    (stem_pre, mid_pre, deep_pre, rise_pre, fb_pool, fb_skip, rb_skip, stem_grad) = rest[9:17]
    (w_stem, w_mid, w_bot, b_mid, b_bot) = rest[17:22]
    rest = rest[22:]
    sums = [
        Summed(full, rest[11 * i : 11 * i + 9], rest[11 * i + 9], rest[11 * i + 10])
        for i, full in enumerate((full0, full1, full2))
    ]

    for item in halo.values():
        item.rows[...] = jnp.zeros(item.rows.shape, BF)
        item.edges[...] = jnp.zeros(item.edges.shape, BF)
    for a in range(w):
        for b in range(d):
            halo["feat"].rows[a + 1, b + 1] = feat[a, b]
            halo["cot"].rows[a + 1, b + 1] = cot[a, b]

    barrier = pltpu.get_barrier_semaphore()
    for target, can_send, _ in halo["feat"].copies(False):
        Halo.guarded(
            can_send,
            functools.partial(
                pl.semaphore_signal, barrier, 1, device_id=target, device_id_type=pl.DeviceIdType.MESH
            ),
        )
    others = 0
    for name in ("dep", "hgt"):
        i, n = lax.axis_index(name), lax.axis_size(name)
        for k in range(1, n):
            other = lax.rem(i + k, n)
            far = jnp.logical_or(other - i > 1, i - other > 1)
            if n > 2:
                Halo.guarded(
                    [far],
                    functools.partial(
                        pl.semaphore_signal, barrier, 1, device_id=at(name, other), device_id_type=pl.DeviceIdType.MESH
                    ),
                )
        others = others + n - (1 + jnp.minimum(i, 1) + jnp.minimum(n - 1 - i, 1))
    peers = 1
    for name in ("wid", "dep", "hgt"):
        i, n = lax.axis_index(name), lax.axis_size(name)
        peers = peers * (1 + jnp.minimum(i, 1) + jnp.minimum(n - 1 - i, 1))
    pl.semaphore_wait(barrier, peers - 1 + others)

    lanes = h
    pool = pattern(lanes, lambda r, c: r // 2 == c)
    pool_mean = (pool / 8.0).astype(BF)
    pool_sum = pool.astype(BF)
    spread = pattern(lanes, lambda r, c: c // 2 == r)
    spread_mean = (spread / 8.0).astype(BF)
    spread = spread.astype(BF)

    def stack_shifts(name, target):
        item = halo[name]
        for a in range(item.w + 2):
            for b in range(item.d + 2):
                target[a, b] = jnp.concatenate(item.shifted(a, b), axis=0)

    def stack_pair(coarse, fine, target):
        up, low = halo[coarse], halo[fine]
        for a in range(low.w + 2):
            for b in range(low.d + 2):
                one = up.shifted((a + 1) // 2, (b + 1) // 2, spread)
                two = low.shifted(a, b)
                target[a, b] = jnp.concatenate([v for pair in zip(one, two) for v in pair], axis=0)

    def patch(source, a, b, pair):
        parts = []
        for q in range(pair):
            parts.append(
                jnp.concatenate([source[a + ka, b + kb + q] for ka in range(3) for kb in range(3)], axis=0)
            )
        return parts[0] if pair == 1 else jnp.concatenate(parts, axis=1)

    def over_rows(span, body):
        pair = 4 if span[1] % 4 == 0 else 2 if span[1] % 2 == 0 else 1
        across = span[1] // pair

        def trip(i, _):
            body(i // across, (i % across) * pair, pair)
            return 0

        count = span[0] * across
        if count == 1:
            body(0, 0, pair)
        else:
            lax.fori_loop(0, count, trip, 0)

    def conv(source, weight, span, store):
        def body(a, b, pair):
            result = mm(weight[...], patch(source, a, b, pair))
            for q in range(pair):
                store(a, b + q, result[:, q * lanes : (q + 1) * lanes])

        over_rows(span, body)

    def wgrad_into(base, patches, grad, width):
        groups = lanes // width
        count = patches.shape[0] // groups
        value = None
        for g in range(groups):
            pieces = [jnp.zeros_like(grad)] * groups
            pieces[g] = grad
            full = pieces[0] if groups == 1 else jnp.concatenate(pieces, axis=0)
            piece = mm_nt(patches[g * count : (g + 1) * count], full)
            value = piece if value is None else value + piece
        where = sums[base[0]].total
        where[base[1] : base[1] + count] += value

    def grad_row(ref, a, b, pair, pad):
        parts = [ref[a + pad, b + pad + q] for q in range(pair)]
        return parts[0] if pair == 1 else jnp.concatenate(parts, axis=1)

    sizes = [27 * f0 * f0, 27 * f0 * f1, 27 * f1 * f2, 27 * (f2 + f1) * f1, 27 * (f1 + f0) * f0]
    rows_of = [v // lanes for v in sizes]
    bases = {i: (seg, sum(rows_of[j] for j in SEGMENTS[seg][: SEGMENTS[seg].index(i)])) for seg in range(3) for i in SEGMENTS[seg]}
    for item in sums:
        item.total[...] = jnp.zeros(item.total.shape, F32)

    halo["feat"].start()
    halo["cot"].start()
    for raw, target in ((raw_stem, w_stem), (raw_mid, w_mid), (raw_bot, w_bot)):
        target[...] = raw[...].reshape(-1, raw.shape[2]).T
    for raw, target in ((raw_mid, b_mid), (raw_bot, b_bot)):
        taps, _, width = raw.shape
        for k in range(taps):
            target[:, k * width : (k + 1) * width] = raw[taps - 1 - k]
    halo["feat"].wait()
    stack_shifts("feat", s_feat)

    def stem_store(a, b, value):
        stem_pre[a, b] = value
        halo["stem"].rows[a + 1, b + 1] = silu(value).astype(BF)

    conv(s_feat, w_stem, spans[0], stem_store)

    def pooled(fine, coarse):
        low, up = halo[fine], halo[coarse]
        for a in range(up.w):
            for b in range(up.d):
                cat = [low.rows[2 * a + 1 + i, 2 * b + 1 + j] for i in range(2) for j in range(2)]
                total = mm(cat[0], pool_mean) + mm(cat[1], pool_mean) + mm(cat[2], pool_mean) + mm(cat[3], pool_mean)
                up.rows[a + 1, b + 1] = total.astype(BF)

    pooled("stem", "half")
    halo["half"].start()
    halo["stem"].start()
    halo["cot"].wait()
    stack_shifts("cot", s_cot)
    fb_pool[...] = jnp.zeros(fb_pool.shape, F32)

    def back_store(a, b, value):
        fb_pool[a // 2, b // 2] += value[:f1]
        fb_skip[a, b] = value[f1:]

    conv(s_cot, b_fin, spans[0], back_store)
    halo["half"].wait()
    stack_shifts("half", s_half)

    def mid_store(a, b, value):
        mid_pre[a, b] = value
        halo["mid"].rows[a + 1, b + 1] = silu(value).astype(BF)

    conv(s_half, w_mid, spans[1], mid_store)
    pooled("mid", "quarter")
    halo["quarter"].start()
    halo["mid"].start()
    halo["quarter"].wait()
    stack_shifts("quarter", s_quarter)

    def deep_store(a, b, value):
        deep_pre[a, b] = value
        halo["deep"].rows[a + 1, b + 1] = silu(value).astype(BF)

    conv(s_quarter, w_bot, spans[2], deep_store)
    halo["deep"].start()
    halo["mid"].wait()
    halo["deep"].wait()
    stack_pair("deep", "mid", s_rise)

    def rise_store(a, b, value):
        rise_pre[a, b] = value
        halo["ra"].rows[a + 1, b + 1] = silu(value).astype(BF)
        grad = mm_split(fb_pool[a, b], pool_sum) * slope(value)
        halo["rg"].rows[a + 1, b + 1] = grad.astype(BF)

    conv(s_rise, w_rise, spans[1], rise_store)
    halo["rg"].start()
    halo["ra"].start()

    def rise_wgrad(a, b, pair):
        wgrad_into(bases[3], patch(s_rise, a, b, pair), grad_row(halo["rg"].rows, a, b, pair, 1), f1)

    over_rows(spans[1], rise_wgrad)
    sums[0].step()
    halo["rg"].wait()
    stack_shifts("rg", s_rg)
    deep_sum = [[None] * spans[2][1] for _ in range(spans[2][0])]

    pair1 = 2 if spans[1][1] % 2 == 0 else 1
    for a in range(spans[1][0]):
        for b in range(0, spans[1][1], pair1):
            result = mm(b_rise[...], patch(s_rg, a, b, pair1))
            for q in range(pair1):
                value = result[:, q * lanes : (q + 1) * lanes]
                rb_skip[a, b + q] = value[f2:]
                ap, bt = a // 2, (b + q) // 2
                old = deep_sum[ap][bt]
                deep_sum[ap][bt] = value[:f2] if old is None else old + value[:f2]
    for a in range(spans[2][0]):
        for b in range(spans[2][1]):
            grad = mm_split(deep_sum[a][b], pool_sum) * slope(deep_pre[a, b])
            halo["dg"].rows[a + 1, b + 1] = grad.astype(BF)
    halo["dg"].start()

    def bottom_wgrad(a, b, pair):
        wgrad_into(bases[2], patch(s_quarter, a, b, pair), grad_row(halo["dg"].rows, a, b, pair, 1), f2)

    over_rows(spans[2], bottom_wgrad)
    sums[0].step()
    halo["stem"].wait()
    halo["ra"].wait()
    stack_pair("ra", "stem", s_fin)

    def final(a, b, pair):
        cells = patch(s_fin, a, b, pair)
        result = mm(w_fin[...], cells)
        for q in range(pair):
            output[a, b + q] = result[:, q * lanes : (q + 1) * lanes].astype(BF)
        wgrad_into(bases[4], cells, grad_row(cot, a, b, pair, 0), f0)

    over_rows(spans[0], final)
    sums[1].step()
    sums[0].step()
    halo["dg"].wait()
    stack_shifts("dg", s_dg)

    def quarter_store(a, b, value):
        wide = mm_split(value, spread_mean)
        for i in range(2):
            for j in range(2):
                at_, bt = 2 * a + i, 2 * b + j
                grad = (rb_skip[at_, bt] + wide) * slope(mid_pre[at_, bt])
                halo["mg"].rows[at_ + 1, bt + 1] = grad.astype(BF)

    conv(s_dg, b_bot, spans[2], quarter_store)
    halo["mg"].start()
    sums[1].step()
    sums[0].step()

    def mid_wgrad(a, b, pair):
        wgrad_into(bases[1], patch(s_half, a, b, pair), grad_row(halo["mg"].rows, a, b, pair, 1), f1)

    over_rows(spans[1], mid_wgrad)
    sums[1].step()
    sums[0].step()
    halo["mg"].wait()
    stack_shifts("mg", s_mg)

    def half_store(a, b, value):
        half_out[a, b] = value
        wide = mm_split(value, spread_mean)
        for i in range(2):
            for j in range(2):
                at_, bt = 2 * a + i, 2 * b + j
                grad = (fb_skip[at_, bt] + wide) * slope(stem_pre[at_, bt])
                stem_grad[at_, bt] = grad.astype(BF)

    conv(s_mg, b_mid, spans[1], half_store)
    sums[1].step()
    sums[0].step()

    def stem_wgrad(a, b, pair):
        wgrad_into(bases[0], patch(s_feat, a, b, pair), grad_row(stem_grad, a, b, pair, 0), f0)

    over_rows(spans[0], stem_wgrad)
    sums[2].step()
    sums[0].step()
    sums[1].step()
    sums[2].step()
    sums[1].step()
    sums[2].step()
    sums[1].step()
    for item in (sums[2], sums[0], sums[1]):
        item.finish()
    for item in halo.values():
        item.finish()


def local(features, cotangent, w_stem, w_middle, w_bottom, w_rise, w_final):
    f0, w, d, h = features.shape
    f1, f2 = w_middle.shape[4], w_bottom.shape[4]
    spans = {0: (w, d), 1: (w // 2, d // 2), 2: (w // 4, d // 4)}
    halos = [(f0, 0), (f0, 0), (f0, 0), (f0, 1), (f1, 1), (f1, 2), (f2, 2), (f1, 1), (f1, 1), (f2, 2), (f1, 1)]
    scratch = [pltpu.SemaphoreType.DMA((27 * len(halos),)), pltpu.SemaphoreType.DMA((27 * len(halos),))]
    for c, level in halos:
        a, b = spans[level]
        scratch += [
            pltpu.VMEM((a + 2, b + 2, c, h), BF),
            pltpu.VMEM((2, 3, 3, c, h), BF),
            pltpu.VMEM((c, h), BF),
        ]
    for c, level in [(f0, 0), (f0, 0), (f0, 1), (f1, 2), (f2 + f1, 1), (f1 + f0, 0), (f1, 1), (f2, 2), (f1, 1)]:
        a, b = spans[level]
        scratch.append(pltpu.VMEM((a + 2, b + 2, 3 * c, h), BF))
    for c, level in [(f0, 0), (f1, 1), (f2, 2), (f1, 1), (f1, 1), (f0, 0), (f1, 1)]:
        scratch.append(pltpu.VMEM((*spans[level], c, h), F32))
    scratch.append(pltpu.VMEM((w, d, f0, h), BF))
    for a, b in ((f0, f0), (f1, f0), (f2, f1), (f0, f1), (f1, f2)):
        scratch.append(pltpu.VMEM((a, 27 * b), BF))
    weights = (w_stem, w_middle, w_bottom, w_rise, w_final)
    counts = [lax.axis_size(axis) for axis in Summed.order]
    unit = 16 * math.prod(counts)
    lengths = []
    for members in SEGMENTS:
        rows = -(-sum(weights[i].size // h for i in members) // unit) * unit
        lengths.append(rows)
        for n in counts:
            scratch += [pltpu.VMEM((rows, h), F32), pltpu.VMEM((rows, h), BF), pltpu.VMEM((rows, h), BF)]
            rows //= n
        scratch += [pltpu.SemaphoreType.DMA((6, max(counts))), pltpu.SemaphoreType.DMA((6, max(counts)))]

    def forward(v):
        return v.reshape(-1, v.shape[4]).T

    def backward(v):
        return v[::-1, ::-1, ::-1].reshape(27, v.shape[3], v.shape[4]).transpose(1, 0, 2).reshape(v.shape[3], -1)

    vmem = pl.BlockSpec(memory_space=pltpu.VMEM)
    out, *packed, half_back = pl.pallas_call(
        functools.partial(step_kernel, (f0, f1, f2, w, d, h)),
        out_shape=(
            jax.ShapeDtypeStruct((w, d, f0, h), BF),
            *[jax.ShapeDtypeStruct((rows, h), BF) for rows in lengths],
            jax.ShapeDtypeStruct((w // 2, d // 2, f0, h), F32),
        ),
        in_specs=[vmem] * 9,
        out_specs=(vmem,) * 5,
        scratch_shapes=scratch,
        compiler_params=pltpu.CompilerParams(
            collective_id=0, has_side_effects=True, vmem_limit_bytes=60 << 20
        ),
        name="unet_step",
    )(
        features.transpose(1, 2, 0, 3),
        cotangent.transpose(1, 2, 0, 3),
        *[v.reshape(-1, *v.shape[3:]) for v in weights[:3]],
        *[forward(v) for v in weights[3:]],
        *[backward(v) for v in weights[3:]],
    )
    cells = w * d * h * lax.axis_size("dep") * lax.axis_size("hgt") * lax.axis_size("wid")
    fine, mid, deep = (1.0 / math.sqrt(cells / k) for k in (1.0, 8.0, 64.0))
    scales = (fine, mid, deep, mid, fine)

    def unpack(*refs):
        for members, source in zip(SEGMENTS, refs[:3]):
            base = 0
            for i in members:
                target = refs[3 + i]
                width = target.shape[1]
                rows = target.shape[0] * width // h
                value = source[base : base + rows].astype(F32) * scales[i]
                base += rows
                for g in range(h // width):
                    target[g * rows : (g + 1) * rows] = value[:, g * width : (g + 1) * width]

    flat = pl.pallas_call(
        unpack,
        out_shape=tuple(jax.ShapeDtypeStruct((v.size // v.shape[4], v.shape[4]), F32) for v in weights),
        in_specs=[vmem] * 3,
        out_specs=(vmem,) * 5,
        compiler_params=pltpu.CompilerParams(vmem_limit_bytes=32 << 20),
        name="unpack",
    )(*packed)
    results = [r.reshape(v.shape) for r, v in zip(flat, weights)]
    return (out.transpose(2, 0, 1, 3), *results, half_back[..., : h // 2].transpose(2, 0, 1, 3))


def solution(mesh):
    placed = (P("grp", "wid", "dep", "hgt"), P("grp", "wid", "dep", "hgt"), P(), P(), P(), P(), P())
    grad = P("grp", None, None, None, None)
    return jax.shard_map(
        local,
        mesh=mesh,
        in_specs=placed,
        out_specs=(P("grp", "wid", "dep", "hgt"), grad, grad, grad, grad, grad, P("grp", "wid", "dep", "hgt")),
        check_vma=False,
    )
```

profile of v0, /device:TPU:0, one launch (start us, length us, event | category | flops | bytes accessed | tf_op | source)
XLA Modules:
  0.0 115.8 jit_solution(14220912346380979280)
XLA Ops:
  0.6 0.0 copy-start.4
  0.6 1.0 rev.7
  1.7 0.8 copy.29.refs_8_
  2.5 1.7 %copy_bitcast_fusion = (bf16[4,4,32,128]{3,2,1,0:T(8,128)(2,1)}, bf16[4,4,32,128]{3,2,1,0:T(8,128)(2,1)}) fusion(bf16[32,4,4,128]{3,2,1,0:T(4,128)(2,1)} %param.8, bf16[32,4,4,128]{3,2,1,0:T(4,128)(2,1)} %param.7), kind=kLoop, calls=%fused_computation | loop fusion | bytes 524288 | tf_op jit(solution)/shard_map/transpose | solution.py:593
  4.2 1.1 copy.27
  5.3 0.9 reshape.60
  6.2 0.0 copy-done.4
  6.2 0.1 rev.6
  6.3 1.1 copy.28.refs_7_
  7.4 0.8 copy.26
  8.2 1.4 %reshape.59 = bf16[5184,64]{0,1:T(8,128)(2,1)} reshape(bf16[3,3,3,192,64]{3,2,1,0,4:T(4,128)(2,1)S(1)} %copy.26) | data formatting | bytes 1327104 | tf_op jit(solution)/shard_map/reshape | solution.py:571
  9.6 92.2 %unet_step.1 = (bf16[4,4,32,128]{3,2,1,0:T(8,128)(2,1)}, bf16[2816,128]{1,0:T(8,128)(2,1)}, bf16[2560,128]{1,0:T(8,128)(2,1)}, bf16[768,128]{1,0:T(8,128)(2,1)}, f32[2,2,32,128]{3,2,1,0:T(8,128)}) custom-call(bf16[4,4,32,128]{3,2,1,0:T(8,128)(2,1)} %get-tuple-element.42.refs_0_, bf16[4,4,32,128]{3,2,1,0:T(8,128)(2,1)} %get-tuple-element.41.refs_1_, ...), custom_call_target="tpu_custom_call" | custom-call | tf_op jit(solution)/shard_map/unet_step/pallas_call | solution.py:577
  101.8 1.6 %copy.30 = bf16[32,4,4,128]{3,2,1,0:T(4,128)(2,1)} copy(bf16[32,4,4,128]{3,0,2,1:T(8,128)(2,1)} %bitcast.40) | data formatting | bytes 262144
  103.4 0.8 slice_bitcast_fusion
  104.3 0.7 copy.33
  105.0 0.0 copy-start.1
  105.0 1.1 copy-done.1
  106.1 0.0 copy-start.2
  106.1 1.1 copy-done.2
  107.2 0.0 copy-start.3
  107.2 0.9 copy-done.3
  108.1 1.9 %unpack.1 = (f32[864,32]{1,0:T(8,128)}, f32[864,64]{1,0:T(8,128)}, f32[1728,128]{1,0:T(8,128)}, f32[5184,64]{1,0:T(8,128)S(1)}, f32[2592,32]{1,0:T(8,128)S(1)}) custom-call(bf16[2816,128]{1,0:T(8,128)(2,1)S(1)} %copy-done.1, bf16[2560,128]{1,0:T(8,128)(2,1)S(1)} %copy-done.2, bf16[768,128]{1,0:T(8,128)(2,1)S(1)} %copy-done.3), custom_call_target="tpu_custom_call" | custom-call | tf_op jit(solution)/shard_map/unpack/pallas_call | solution.py:614
  110.0 0.0 copy-start
  110.0 1.1 copy-done
  111.1 2.5 %copy.32 = f32[3,3,3,96,32]{3,4,2,1,0:T(8,128)} copy(f32[3,3,3,96,32]{4,3,2,1,0:T(8,128)} %bitcast.32) | data formatting | bytes 663552
  113.6 2.2 %copy.31 = f32[3,3,3,192,64]{3,4,2,1,0:T(8,128)} copy(f32[3,3,3,192,64]{4,3,2,1,0:T(8,128)S(1)} %bitcast.31) | data formatting | bytes 2654208
Async XLA Ops:
  0.6 5.6 %copy-start.4 = (bf16[3,3,3,192,64]{3,4,2,1,0:T(8,128)(2,1)S(1)}, bf16[3,3,3,192,64]{3,4,2,1,0:T(8,128)(2,1)}, u32[]{:S(2)}) copy-start(bf16[3,3,3,192,64]{3,4,2,1,0:T(8,128)(2,1)} %param.12) | copy-start | bytes 1990660
  105.0 1.1 copy-start.1
  106.1 1.1 copy-start.2
  107.2 0.9 copy-start.3
  110.0 1.1 copy-start
where the time goes:
time: 116 us
  Pallas kernels  94.1 us (81%)
  local copies, waits for them, and re-layouts  21 us (18%)
    pallas_call x1, Pallas kernels, local(): pl.pallas_call(functools.partial(step_kernel, (f0, f1, f2, w, d, h)), out...  92.2 us
    unnamed x16, local copies, waits for them, and re-layouts  13 us
    reshape x2, local copies, waits for them, and re-layouts, forward(): return v.reshape(-1, v.shape[4]).T  2.34 us

commit v1 on v0

v1 whole, which is shorter than its diff:
```python
import functools
import math

import jax
import jax.numpy as jnp
from jax import lax
from jax.experimental import pallas as pl
from jax.experimental.pallas import tpu as pltpu
from jax.sharding import PartitionSpec as P

BF, F32 = jnp.bfloat16, jnp.float32
AXES = ("grp", "dep", "hgt", "wid")
GROUP = ("wid", "hgt", "dep")
TILE = 16


class Names(dict):
    __getattr__ = dict.__getitem__


def spread_out(tree):
    if not isinstance(tree, dict):
        return [tree], lambda leaves: next(leaves)
    parts = {k: spread_out(v) for k, v in tree.items()}
    leaves = [leaf for some, _ in parts.values() for leaf in some]
    return leaves, lambda leaves: Names({k: back(leaves) for k, (_, back) in parts.items()})


def mm(a, b):
    return lax.dot_general(a, b, (((1,), (0,)), ((), ())), preferred_element_type=F32)


def mm_nt(a, b):
    return lax.dot_general(a, b, (((1,), (1,)), ((), ())), preferred_element_type=F32)


def mm_split(a, b):
    high = a.astype(BF)
    low = (a - high.astype(F32)).astype(BF)
    return mm(high, b) + mm(low, b)


def silu(v):
    return v * jax.nn.sigmoid(v)


def slope(v):
    g = jax.nn.sigmoid(v)
    return g * (1.0 + v * (1.0 - g))


def pattern(lanes, test):
    row = lax.broadcasted_iota(jnp.int32, (lanes, lanes), 0)
    col = lax.broadcasted_iota(jnp.int32, (lanes, lanes), 1)
    return jnp.where(test(row, col), 1.0, 0.0)


def neighbours():
    count = 1
    for name in GROUP:
        count *= min(lax.axis_size(name), 3)
    return count - 1


def edge_rows(channels, rows, lanes):
    size = TILE
    while channels % size or rows * (channels // size) > lanes // 2:
        size += TILE
    return size


class Halo:
    def __init__(self, group, rows, edges, own, span, sems):
        self.rows, self.edges, self.own = rows, edges, own
        self.base = group * neighbours()
        self.w, self.d, self.h = span
        self.send, self.recv = sems
        self.before = None
        self.unsent = False
        self.side = own.shape[1] // 2
        self.tall = own.shape[0]
        self.per = rows.shape[2] // self.tall

    def clear(self):
        blank = jnp.zeros(self.rows.shape[2:], BF)
        for a in range(self.w + 2):
            for b in range(self.d + 2):
                if a in (0, self.w + 1) or b in (0, self.d + 1):
                    self.rows[a, b] = blank
        self.edges[...] = jnp.zeros(self.edges.shape, BF)

    def fill_edges(self):
        lane = lax.broadcasted_iota(jnp.int32, self.own.shape, 1)
        tile = jnp.zeros(self.own.shape, F32)
        for a in range(self.w):
            for b in range(self.d):
                row = self.rows[a + 1, b + 1].astype(F32)
                for g in range(self.per):
                    r = (a * self.d + b) * self.per + g
                    part_of = row[g * self.tall : (g + 1) * self.tall]
                    tile = jnp.where(lane == r, part_of[:, 0:1], tile)
                    tile = jnp.where(lane == self.side + r, part_of[:, self.h - 1 : self.h], tile)
        self.own[...] = tile.astype(BF)

    def copies(self):
        place = {name: lax.axis_index(name) for name in AXES}
        size = {name: lax.axis_size(name) for name in AXES}

        def choices(name):
            i, n = place[name], size[name]
            if n == 1:
                return [(0, 0, True, True)]
            if n == 2:
                return [(0, 0, True, True), (1, 1 - 2 * i, True, True)]
            return [(0, 0, True, True), (1, 1, i < n - 1, i > 0), (2, -1, i > 0, i < n - 1)]

        def cells(step, code, count):
            if code == 0:
                return pl.ds(1, count), pl.ds(1, count)
            up = (1 + step) // 2
            return pl.ds(1 + (count - 1) * up, 1), pl.ds((count + 1) * (1 - up), 1)

        out = []
        for cw, sw, ow, iw in choices("wid"):
            for cd, sd, od, id_ in choices("dep"):
                for ch, sh, oh, ih in choices("hgt"):
                    if cw == 0 and cd == 0 and ch == 0:
                        continue
                    slot = self.base + len(out)
                    target = {"wid": place["wid"] + sw, "dep": place["dep"] + sd, "hgt": place["hgt"] + sh}
                    if ch == 0:
                        from_w, to_w = cells(sw, cw, self.w)
                        from_d, to_d = cells(sd, cd, self.d)
                        source = self.rows.at[from_w, from_d]
                        dest = self.rows.at[to_w, to_d]
                    else:
                        source = self.own
                        dest = self.edges.at[(1 - sh) // 2, 1 - sw, 1 - sd]
                    copy = pltpu.make_async_remote_copy(
                        src_ref=source,
                        dst_ref=dest,
                        send_sem=self.send.at[slot],
                        recv_sem=self.recv.at[slot],
                        device_id=target,
                        device_id_type=pl.DeviceIdType.MESH,
                    )
                    out.append((copy, [c for c in (ow, od, oh) if c is not True], [c for c in (iw, id_, ih) if c is not True]))
        return out

    @staticmethod
    def guarded(conditions, action):
        if not conditions:
            action()
        else:
            pl.when(functools.reduce(jnp.logical_and, conditions))(action)

    def start(self):
        if self.before is not None:
            self.before.finish()
        self.fill_edges()
        for copy, can_send, _ in self.copies():
            self.guarded(can_send, copy.start)
        self.unsent = True

    def wait(self):
        for copy, _, can_take in self.copies():
            self.guarded(can_take, copy.wait_recv)

    def finish(self):
        if self.unsent:
            for copy, can_send, _ in self.copies():
                self.guarded(can_send, copy.wait_send)
        self.unsent = False

    def shifted(self, a, b, spread=None):
        lanes = self.own.shape[1]
        h = self.h if spread is None else 2 * self.h
        row = self.rows[a, b]
        if spread is not None:
            row = mm(row, spread).astype(BF)
        dw = 0 if a == 0 else 2 if a == self.w + 1 else 1
        dd = 0 if b == 0 else 2 if b == self.d + 1 else 1
        r = ((self.w - 1, a - 1, 0)[dw] * self.d + (self.d - 1, b - 1, 0)[dd]) * self.per

        lane = lax.broadcasted_iota(jnp.int32, (self.tall, lanes), 1)
        low, high = self.edges[0, dw, dd].astype(F32), self.edges[1, dw, dd].astype(F32)
        wide = row.astype(F32)
        befores, afters = [], []
        for g in range(self.per):
            here = wide[g * self.tall : (g + 1) * self.tall]
            left = low[:, self.side + r + g : self.side + r + g + 1]
            right = high[:, r + g : r + g + 1]
            before = jnp.where(lane == 0, left, pltpu.roll(here, 1, 1))
            after = jnp.where(lane == h - 1, right, pltpu.roll(here, lanes - 1, 1))
            if h < lanes:
                before = jnp.where(lane < h, before, 0.0)
                after = jnp.where(lane < h, after, 0.0)
            befores.append(before.astype(BF))
            afters.append(after.astype(BF))
        if self.per == 1:
            return befores[0], row, afters[0]
        return jnp.concatenate(befores, axis=0), row, jnp.concatenate(afters, axis=0)


def part(i, m):
    return pl.ds(pl.multiple_of(i * m, TILE), m)


def position(axes):
    place, count = 0, 1
    for axis in axes:
        place = place * lax.axis_size(axis) + lax.axis_index(axis)
        count *= lax.axis_size(axis)
    return place, count


def device_at(axes, place):
    where = {name: lax.axis_index(name) for name in GROUP}
    for axis in axes[::-1]:
        n = lax.axis_size(axis)
        where[axis] = place if axis == axes[0] else lax.rem(place, n)
        place = lax.div(place, n)
    return where


class Summed:
    def __init__(self, order, full, buffers, send, recv):
        self.order, self.full = order, full
        self.levels = [buffers[3 * i : 3 * i + 3] for i in range(len(order))]
        self.total = buffers[0]
        self.send, self.recv = send, recv
        self.stage, self.open, self.sent = 0, None, []

    def copy(self, stage, axes, source, dest, to):
        return pltpu.make_async_remote_copy(
            src_ref=source,
            dst_ref=dest,
            send_sem=self.send.at[stage],
            recv_sem=self.recv.at[stage],
            device_id=device_at(axes, to),
            device_id_type=pl.DeviceIdType.MESH,
        )

    def exchange(self, stage, axes, pieces, whole, m):
        i, n = position(axes)
        if n == 1:
            return
        for k in range(1, n):
            to = lax.rem(i + k, n)
            source, dest = pieces(to, i)
            self.copy(stage, axes, source, dest, to).start()
        every = whole.at[pl.ds(0, (n - 1) * m)]
        self.open = self.copy(stage, axes, every, every, lax.rem(i + 1, n))
        self.sent.append(self.open)

    def step(self):
        stage, deep = self.stage, len(self.order)
        self.stage += 1
        if self.open is not None:
            self.open.wait_recv()
            self.open = None
        if 0 < stage <= deep:
            i, n = position(self.order[stage - 1])
            held, _, came = self.levels[stage - 1]
            m = held.shape[0] // n
            value = held[part(i, m)]
            for k in range(1, n):
                value = value + came[part(lax.rem(i + k, n), m)].astype(F32)
            if stage < deep:
                self.levels[stage][0][...] = value
            else:
                place, _ = position([axis for axes in self.order for axis in axes])
                self.full[part(place, m)] = value.astype(BF)
        if stage < deep:
            held, wire, came = self.levels[stage]
            i, n = position(self.order[stage])
            m = held.shape[0] // n
            for k in range(1, n):
                there = part(lax.rem(i + k, n), m)
                wire[there] = held[there].astype(BF)
            self.exchange(stage, self.order[stage], lambda to, me: (wire.at[part(to, m)], came.at[part(me, m)]), came, m)
        elif stage < 2 * deep:
            depth = 2 * deep - stage
            place, count = position([axis for axes in self.order[:depth] for axis in axes])
            m = self.full.shape[0] // count
            piece = self.full.at[part(place, m)]
            self.exchange(stage, self.order[depth - 1], lambda to, me: (piece, piece), self.full, m)

    def finish(self):
        while self.stage <= 2 * len(self.order):
            self.step()
        for copy in self.sent:
            copy.wait_send()


HALOS = dict(
    feat=(0, 0, 0), half=(0, 1, 1), quarter=(1, 2, 0), deep=(2, 2, 1), rg=(1, 1, 0), dg=(2, 2, 1),
    mg=(1, 1, 0), cot=(0, 0, 2), mid=(1, 1, 2), stem=(0, 0, 3), ra=(1, 1, 3),
)
STACKS = dict(
    feat=(0, 0), cot=(0, 0), half=(0, 1), quarter=(1, 2), up2=(2, 1), mid=(1, 1), up1=(1, 0),
    stem=(0, 0), rg=(1, 1), dg=(2, 2), mg=(1, 1),
)


def blocks(size, lanes):
    return -(-size // lanes)


def segments(f, lanes):
    f0, f1, f2 = f
    return dict(
        low=[(f1, blocks(27 * f1, lanes))],
        up=[(f1, blocks(27 * f2, lanes))],
        bot=[(27 * f1, blocks(f2, lanes))],
        fin=[(3 * f0, blocks(9 * f1, lanes)), (3 * f0, blocks(9 * f0, lanes))],
        mid=[(f1, blocks(27 * f0, lanes))],
        stem=[(f0, blocks(27 * f0, lanes))],
    )


STAGED = (("wid",), ("hgt",), ("dep",))


def orders():
    whole = math.prod(lax.axis_size(axis) for axis in GROUP)
    near = (GROUP,) if whole <= 16 else STAGED
    return dict(low=STAGED, up=STAGED, bot=STAGED, fin=STAGED, mid=near, stem=near)


def step_kernel(cfg, back, *refs):
    (f0, f1, f2, w, d, h) = cfg
    ref = back(iter(refs))
    spans = {0: (w, d, h), 1: (w // 2, d // 2, h // 2), 2: (w // 4, d // 4, h // 4)}
    lanes = h
    halo = Names()
    last = {}
    for name, (_, level, group) in HALOS.items():
        own = ref.halos[name]
        halo[name] = Halo(group, own.rows, own.edges, own.own, spans[level], (ref.send, ref.recv))
        halo[name].before = last.get(group)
        last[group] = halo[name]
    stacks = ref.stacks
    sums = Names()
    for name, order in orders().items():
        own = ref.sums[name]
        sums[name] = Summed(order, ref.outs[name], list(own.levels.values()), own.send, own.recv)

    loads = Names()
    for i, name in enumerate(ref.ins):
        loads[name] = pltpu.make_async_copy(ref.ins[name], ref.inside[name], ref.load.at[i])
        loads[name].start()
    for item in halo.values():
        item.clear()

    def take(load, source, item):
        load.wait()
        ref.wide[...] = source[...].astype(F32)
        for a in range(w):
            for b in range(d):
                item.rows[a + 1, b + 1] = ref.wide[pl.ds(a * d + b, f0, stride=w * d), :].astype(BF)

    take(loads.feat, ref.inside.feat, halo.feat)
    barrier = pltpu.get_barrier_semaphore()
    me, everyone = position(GROUP)
    for k in range(1, everyone):
        pl.semaphore_signal(
            barrier, 1, device_id=device_at(GROUP, lax.rem(me + k, everyone)), device_id_type=pl.DeviceIdType.MESH
        )
    pl.semaphore_wait(barrier, everyone - 1)

    halo.feat.start()
    take(loads.cot, ref.inside.cot, halo.cot)
    halo.cot.start()
    pool = pattern(lanes, lambda r, c: r // 2 == c)
    pool_mean = (pool / 8.0).astype(BF)
    pool_sum = pool.astype(BF)
    spread = pattern(lanes, lambda r, c: c // 2 == r)
    spread_mean = (spread / 8.0).astype(BF)
    spread = spread.astype(BF)

    def forward(raw, target):
        target[...] = raw[...].reshape(-1, raw.shape[2]).T

    def side_by_side(raw, target, low, high):
        width = high - low
        for k in range(raw.shape[0]):
            target[:, k * width : (k + 1) * width] = raw[k][:, low:high]

    loads.stem.wait()
    forward(ref.inside.stem, ref.w_stem)
    loads.fin.wait()
    forward(ref.inside.fin, ref.b_fin)
    side_by_side(ref.inside.fin, ref.w_fin_up, 0, f1)
    side_by_side(ref.inside.fin, ref.w_fin_low, f1, f1 + f0)
    loads.mid.wait()
    forward(ref.inside.mid, ref.w_mid)
    side_by_side(ref.inside.mid, ref.b_mid, 0, f1)
    loads.bot.wait()
    forward(ref.inside.bot, ref.w_bot)
    side_by_side(ref.inside.bot, ref.b_bot, 0, f2)
    loads.rise.wait()
    forward(ref.inside.rise, ref.b_rise)
    side_by_side(ref.inside.rise, ref.w_rise_up, 0, f2)
    side_by_side(ref.inside.rise, ref.w_rise_low, f2, f2 + f1)

    def stack(item, target, back=False):
        for a in range(item.w + 2):
            for b in range(item.d + 2):
                parts = item.shifted(a, b)
                target[a, b] = jnp.concatenate(parts[::-1] if back else parts, axis=0)

    def stack_up(up, target):
        for a in range(target.shape[0]):
            for b in range(target.shape[1]):
                target[a, b] = jnp.concatenate(up.shifted((a + 1) // 2, (b + 1) // 2, spread), axis=0)

    def patch(source, a, b, pair, back=False, middle=False):
        third = source.shape[2] // 3
        rows = slice(third, 2 * third) if middle else slice(0, 3 * third)
        parts = []
        for q in range(pair):
            taps = [(ka, kb) for ka in range(3) for kb in range(3)]
            parts.append(
                jnp.concatenate([source[a + ka, b + kb + q, rows] for ka, kb in (taps[::-1] if back else taps)], axis=0)
            )
        return parts[0] if pair == 1 else jnp.concatenate(parts, axis=1)

    def over_rows(span, body):
        pair = 4 if span[1] % 4 == 0 else 2 if span[1] % 2 == 0 else 1
        across = span[1] // pair

        def trip(i, _):
            body(i // across, (i % across) * pair, pair)
            return 0

        count = span[0] * across
        if count <= 2:
            for i in range(count):
                trip(i, 0)
        else:
            lax.fori_loop(0, count, trip, 0)

    def conv(source, weight, span, store, back=False):
        def body(a, b, pair):
            result = mm(weight[...], patch(source, a, b, pair, back))
            for q in range(pair):
                store(a, b + q, result[:, q * lanes : (q + 1) * lanes])

        over_rows(span, body)

    def put_blocks(where, base, value):
        rows, width = value.shape
        count = blocks(width, lanes)
        if count * lanes > width:
            value = jnp.concatenate([value, jnp.zeros((rows, count * lanes - width), value.dtype)], axis=1)
        for j in range(count):
            where[base + j * rows : base + (j + 1) * rows] = value[:, j * lanes : (j + 1) * lanes]

    def beside(span, pick):
        return jnp.concatenate([pick(a, b) for a in range(span[0]) for b in range(span[1])], axis=1)

    halo.feat.wait()
    stack(halo.feat, stacks.feat)

    def stem_store(a, b, value):
        ref.stem_pre[a, b] = value
        halo.stem.rows[a + 1, b + 1] = silu(value).astype(BF)

    conv(stacks.feat, ref.w_stem, spans[0], stem_store)

    def pooled(fine, coarse):
        low, up = fine, coarse
        for a in range(up.w):
            for b in range(up.d):
                cat = [low.rows[2 * a + 1 + i, 2 * b + 1 + j] for i in range(2) for j in range(2)]
                total = mm(cat[0], pool_mean) + mm(cat[1], pool_mean) + mm(cat[2], pool_mean) + mm(cat[3], pool_mean)
                up.rows[a + 1, b + 1] = total.astype(BF)

    pooled(halo.stem, halo.half)
    halo.cot.wait()
    halo.half.start()
    halo.stem.start()
    stack(halo.cot, stacks.cot, back=True)
    ref.fb_pool[...] = jnp.zeros(ref.fb_pool.shape, F32)

    def back_store(a, b, value):
        ref.fb_pool[a // 2, b // 2] += value[:f1]
        ref.fb_skip[a, b] = value[f1:]

    conv(stacks.cot, ref.b_fin, spans[0], back_store, back=True)
    for a in range(spans[1][0]):
        for b in range(spans[1][1]):
            ref.fb_pool[a, b] = mm_split(ref.fb_pool[a, b], pool_sum)
    halo.half.wait()
    stack(halo.half, stacks.half)

    def mid_store(a, b, value):
        ref.mid_pre[a, b] = value
        halo.mid.rows[a + 1, b + 1] = silu(value).astype(BF)

    conv(stacks.half, ref.w_mid, spans[1], mid_store)
    pooled(halo.mid, halo.quarter)
    halo.quarter.start()
    halo.mid.start()
    halo.stem.wait()
    stack(halo.stem, stacks.stem)

    def final_low(a, b, value):
        ref.fin_part[a, b] = value

    conv(stacks.stem, ref.w_fin_low, spans[0], final_low)
    cot_cells = lambda: beside(spans[0], lambda a, b: stacks.cot[a + 1, b + 1])
    low_cells = beside(spans[0], lambda a, b: patch(stacks.stem, a, b, 1, middle=True))
    put_blocks(sums.fin.total, 3 * f0 * blocks(9 * f1, lanes), mm_nt(cot_cells(), low_cells))
    halo.quarter.wait()
    stack(halo.quarter, stacks.quarter)

    def deep_store(a, b, value):
        ref.deep_pre[a, b] = value
        halo.deep.rows[a + 1, b + 1] = silu(value).astype(BF)

    conv(stacks.quarter, ref.w_bot, spans[2], deep_store)
    halo.deep.start()
    halo.mid.wait()
    stack(halo.mid, stacks.mid)

    def rise_low(a, b, value):
        ref.rise_pre[a, b] = value

    conv(stacks.mid, ref.w_rise_low, spans[1], rise_low)
    halo.deep.wait()
    stack_up(halo.deep, stacks.up2)

    def rise_store(a, b, value):
        value = value + ref.rise_pre[a, b]
        halo.ra.rows[a + 1, b + 1] = silu(value).astype(BF)
        grad = ref.fb_pool[a, b] * slope(value)
        halo.rg.rows[a + 1, b + 1] = grad.astype(BF)

    conv(stacks.up2, ref.w_rise_up, spans[1], rise_store)
    halo.rg.start()
    halo.ra.start()

    grad1 = lambda item: beside(spans[1], lambda a, b: item.rows[a + 1, b + 1])

    def wide_wgrad(segment, grad, source, span):
        cells = beside(span, lambda a, b: patch(source, a, b, 1))
        put_blocks(segment.total, 0, mm_nt(grad, cells))

    wide_wgrad(sums.low, grad1(halo.rg), stacks.mid, spans[1])
    sums.low.step()
    wide_wgrad(sums.up, grad1(halo.rg), stacks.up2, spans[1])
    sums.up.step()
    sums.low.step()
    halo.rg.wait()
    stack(halo.rg, stacks.rg, back=True)
    deep_sum = [[None] * spans[2][1] for _ in range(spans[2][0])]
    pair1 = 2 if spans[1][1] % 2 == 0 else 1
    for a in range(spans[1][0]):
        for b in range(0, spans[1][1], pair1):
            result = mm(ref.b_rise[...], patch(stacks.rg, a, b, pair1, back=True))
            for q in range(pair1):
                value = result[:, q * lanes : (q + 1) * lanes]
                ref.rb_skip[a, b + q] = value[f2:]
                ap, bt = a // 2, (b + q) // 2
                old = deep_sum[ap][bt]
                deep_sum[ap][bt] = value[:f2] if old is None else old + value[:f2]
    for a in range(spans[2][0]):
        for b in range(spans[2][1]):
            grad = mm_split(deep_sum[a][b], pool_sum) * slope(ref.deep_pre[a, b])
            halo.dg.rows[a + 1, b + 1] = grad.astype(BF)
    halo.dg.start()
    sums.up.step()
    cells2 = beside(spans[2], lambda a, b: patch(stacks.quarter, a, b, 1))
    grad2 = beside(spans[2], lambda a, b: halo.dg.rows[a + 1, b + 1])
    bot = mm_nt(cells2, grad2)
    put_blocks(sums.bot.total, 0, bot)
    sums.bot.step()
    halo.ra.wait()
    stack_up(halo.ra, stacks.up1)
    sums.low.step()
    up_cells = beside(spans[0], lambda a, b: patch(stacks.up1, a, b, 1, middle=True))
    put_blocks(sums.fin.total, 0, mm_nt(cot_cells(), up_cells))
    sums.fin.step()
    halo.dg.wait()
    stack(halo.dg, stacks.dg, back=True)

    def quarter_store(a, b, value):
        wide = mm_split(value, spread_mean)
        for i in range(2):
            for j in range(2):
                at_, bt = 2 * a + i, 2 * b + j
                grad = (ref.rb_skip[at_, bt] + wide) * slope(ref.mid_pre[at_, bt])
                halo.mg.rows[at_ + 1, bt + 1] = grad.astype(BF)

    conv(stacks.dg, ref.b_bot, spans[2], quarter_store, back=True)
    halo.mg.start()
    wide_wgrad(sums.mid, grad1(halo.mg), stacks.half, spans[1])
    sums.mid.step()
    sums.up.step()
    sums.bot.step()
    sums.fin.step()
    sums.low.step()
    halo.mg.wait()
    stack(halo.mg, stacks.mg, back=True)

    def half_store(a, b, value):
        ref.half_wide[pl.ds(a * spans[1][1] + b, f0, stride=spans[1][0] * spans[1][1]), :] = value
        wide = mm_split(value, spread_mean)
        for i in range(2):
            for j in range(2):
                at_, bt = 2 * a + i, 2 * b + j
                grad = (ref.fb_skip[at_, bt] + wide) * slope(ref.stem_pre[at_, bt])
                ref.stem_grad[at_, bt] = grad.astype(BF)

    conv(stacks.mg, ref.b_mid, spans[1], half_store, back=True)
    ref.outs.half[...] = ref.half_wide[...]
    wide_wgrad(sums.stem, beside(spans[0], lambda a, b: ref.stem_grad[a, b]), stacks.feat, spans[0])
    sums.stem.step()
    sums.up.step()
    sums.bot.step()
    sums.fin.step()
    sums.low.step()
    sums.mid.step()

    def final_store(a, b, value):
        ref.wide[pl.ds(a * d + b, f0, stride=w * d), :] = ref.fin_part[a, b] + value

    conv(stacks.up1, ref.w_fin_up, spans[0], final_store)
    ref.outs.output[...] = ref.wide[...].astype(BF)
    sums.stem.step()
    sums.up.step()
    sums.bot.step()
    sums.fin.step()
    sums.low.step()
    sums.mid.step()
    sums.up.step()
    sums.stem.step()
    sums.bot.step()
    sums.fin.step()
    sums.low.step()
    sums.up.step()
    sums.bot.step()
    sums.fin.step()
    for item in sums.values():
        item.finish()
    for item in halo.values():
        item.finish()


def unpack_kernel(cfg, back, *refs):
    (f0, f1, f2, lanes, scales) = cfg
    ref = back(iter(refs))
    loads = Names()
    for i, name in enumerate(ref.ins):
        loads[name] = pltpu.make_async_copy(ref.ins[name], ref.inside[name], ref.load.at[i])
        loads[name].start()
    stores = []

    def send(source, target):
        copy = pltpu.make_async_copy(source, target, ref.store.at[len(stores)])
        copy.start()
        stores.append(copy)

    def side(source, base, rows, width, scale):
        count = blocks(width, lanes)
        value = [source[base + j * rows : base + (j + 1) * rows].astype(F32) * scale for j in range(count)]
        return jnp.concatenate(value, axis=1)

    loads.output.wait()
    send(ref.inside.output, ref.outs.output)
    loads.half.wait()
    ref.ready.half[...] = ref.inside.half[:, : lanes // 2]
    send(ref.ready.half, ref.outs.half)
    loads.low.wait()
    loads.up.wait()
    low = side(ref.inside.low, 0, f1, 27 * f1, scales.rise)
    up = side(ref.inside.up, 0, f1, 27 * f2, scales.rise)
    for k in range(27):
        ref.ready.rise[k] = jnp.concatenate([up[:, k * f2 : (k + 1) * f2], low[:, k * f1 : (k + 1) * f1]], axis=1)
    send(ref.ready.rise, ref.outs.rise)
    loads.bot.wait()
    ref.ready.bot[...] = side(ref.inside.bot, 0, 27 * f1, f2, scales.bot)[:, :f2]
    send(ref.ready.bot, ref.outs.bot)
    loads.fin.wait()
    up = side(ref.inside.fin, 0, 3 * f0, 9 * f1, scales.fin)
    low = side(ref.inside.fin, 3 * f0 * blocks(9 * f1, lanes), 3 * f0, 9 * f0, scales.fin)
    for k in range(27):
        at_, rows = k // 3, slice((k % 3) * f0, (k % 3 + 1) * f0)
        ref.ready.fin[k] = jnp.concatenate([up[rows, at_ * f1 : (at_ + 1) * f1], low[rows, at_ * f0 : (at_ + 1) * f0]], axis=1)
    send(ref.ready.fin, ref.outs.fin)
    for load, source, target, out, scale in (
        (loads.mid, ref.inside.mid, ref.ready.mid, ref.outs.mid, scales.mid),
        (loads.stem, ref.inside.stem, ref.ready.stem, ref.outs.stem, scales.stem),
    ):
        load.wait()
        width = target.shape[1]
        for j in range(blocks(27 * f0, lanes)):
            value = (source[j * width : (j + 1) * width].astype(F32) * scale).T
            rows = min(lanes, 27 * f0 - j * lanes)
            target[j * lanes : j * lanes + rows] = value[:rows]
        send(target, out)
    for copy in stores:
        copy.wait()


def local(features, cotangent, w_stem, w_middle, w_bottom, w_rise, w_final):
    f0, w, d, h = features.shape
    f1, f2 = w_middle.shape[4], w_bottom.shape[4]
    f = (f0, f1, f2)
    spans = {0: (w, d), 1: (w // 2, d // 2), 2: (w // 4, d // 4)}
    near = neighbours()
    sets = 1 + max(group for _, _, group in HALOS.values())
    flat = w * d * f0
    inputs = dict(
        feat=features.reshape(flat, h),
        cot=cotangent.reshape(flat, h),
        stem=w_stem.reshape(27, f0, f0),
        fin=w_final.transpose(0, 1, 2, 4, 3).reshape(27, f0, f1 + f0),
        mid=w_middle.reshape(27, f0, f1),
        bot=w_bottom.reshape(27, f1, f2),
        rise=w_rise.transpose(0, 1, 2, 4, 3).reshape(27, f1, f2 + f1),
    )
    outs = dict(output=jax.ShapeDtypeStruct((flat, h), BF), half=jax.ShapeDtypeStruct((flat // 4, h), F32))
    halos, sums = {}, {}
    for name, (c, level, _) in HALOS.items():
        a, b = spans[level]
        tall = edge_rows(f[c], a * b, h)
        halos[name] = dict(
            rows=pltpu.VMEM((a + 2, b + 2, f[c], h), BF),
            edges=pltpu.VMEM((2, 3, 3, tall, h), BF),
            own=pltpu.VMEM((tall, h), BF),
        )
    place = segments(f, h)
    for name, order in orders().items():
        unit = TILE * math.prod(lax.axis_size(axis) for axis in GROUP)
        rows = -(-sum(a * b for a, b in place[name]) // unit) * unit
        outs[name] = jax.ShapeDtypeStruct((rows, h), BF)
        levels = {}
        for i, axes in enumerate(order):
            for j, kind in enumerate((F32, BF, BF)):
                levels[3 * i + j] = pltpu.VMEM((rows, h), kind)
            rows //= math.prod(lax.axis_size(axis) for axis in axes)
        several = pltpu.SemaphoreType.DMA((2 * len(order),))
        sums[name] = dict(levels=levels, send=several, recv=several)

    def cells_of(c, level, kind=F32):
        return pltpu.VMEM((*spans[level], c, h), kind)

    def taps(a, b):
        return pltpu.VMEM((a, 27 * b), BF)

    scratch = dict(
        send=pltpu.SemaphoreType.DMA((sets * near,)),
        recv=pltpu.SemaphoreType.DMA((sets * near,)),
        load=pltpu.SemaphoreType.DMA((len(inputs),)),
        inside={name: pltpu.VMEM(v.shape, BF) for name, v in inputs.items()},
        halos=halos,
        sums=sums,
        stacks={
            name: pltpu.VMEM((spans[level][0] + 2, spans[level][1] + 2, 3 * f[c], h), BF)
            for name, (c, level) in STACKS.items()
        },
        stem_pre=cells_of(f0, 0), mid_pre=cells_of(f1, 1), deep_pre=cells_of(f2, 2), rise_pre=cells_of(f1, 1),
        fb_pool=cells_of(f1, 1), fb_skip=cells_of(f0, 0), rb_skip=cells_of(f1, 1), fin_part=cells_of(f0, 0),
        stem_grad=cells_of(f0, 0, BF),
        wide=pltpu.VMEM((flat, h), F32), half_wide=pltpu.VMEM((flat // 4, h), F32),
        w_stem=taps(f0, f0), w_mid=taps(f1, f0), w_bot=taps(f2, f1), w_rise_up=taps(f1, f2), w_rise_low=taps(f1, f1),
        w_fin_up=taps(f0, f1), w_fin_low=taps(f0, f0), b_mid=taps(f0, f1), b_bot=taps(f1, f2),
        b_rise=taps(f2 + f1, f1), b_fin=taps(f1 + f0, f0),
    )
    vmem = pl.BlockSpec(memory_space=pltpu.VMEM)
    anywhere = pl.BlockSpec(memory_space=pl.ANY)
    leaves, back = spread_out(dict(ins=inputs, outs=outs, **scratch))
    done = pl.pallas_call(
        functools.partial(step_kernel, (f0, f1, f2, w, d, h), back),
        out_shape=tuple(outs.values()),
        in_specs=[anywhere] * len(inputs),
        out_specs=(vmem,) * len(outs),
        scratch_shapes=leaves[len(inputs) + len(outs) :],
        compiler_params=pltpu.CompilerParams(collective_id=0, has_side_effects=True, vmem_limit_bytes=60 << 20),
        name="unet_step",
    )(*inputs.values())
    packed = dict(zip(outs, done))
    cells = w * d * h * math.prod(lax.axis_size(axis) for axis in GROUP)
    fine, mid, deep = (1.0 / math.sqrt(cells / k) for k in (1.0, 8.0, 64.0))
    scales = Names(stem=fine, mid=mid, bot=deep, rise=mid, fin=fine)

    results = dict(
        output=jax.ShapeDtypeStruct((flat, h), BF),
        stem=jax.ShapeDtypeStruct((27 * f0, f0), F32),
        mid=jax.ShapeDtypeStruct((27 * f0, f1), F32),
        bot=jax.ShapeDtypeStruct((27 * f1, f2), F32),
        rise=jax.ShapeDtypeStruct((27, f1, f2 + f1), F32),
        fin=jax.ShapeDtypeStruct((27, f0, f1 + f0), F32),
        half=jax.ShapeDtypeStruct((flat // 4, h // 2), F32),
    )
    hold = dict(
        inside={n: pltpu.VMEM(v.shape, v.dtype) for n, v in packed.items()},
        ready={n: pltpu.VMEM(v.shape, v.dtype) for n, v in results.items()},
        load=pltpu.SemaphoreType.DMA((len(packed),)),
        store=pltpu.SemaphoreType.DMA((len(results),)),
    )
    leaves, back = spread_out(dict(ins=packed, outs=results, **hold))
    final = pl.pallas_call(
        functools.partial(unpack_kernel, (f0, f1, f2, h, scales), back),
        out_shape=tuple(results.values()),
        in_specs=[anywhere] * len(packed),
        out_specs=(anywhere,) * len(results),
        scratch_shapes=leaves[len(packed) + len(results) :],
        compiler_params=pltpu.CompilerParams(vmem_limit_bytes=60 << 20),
        name="unpack",
    )(*packed.values())
    final = Names(zip(results, final))
    return (
        final.output.reshape(f0, w, d, h),
        final.stem.reshape(w_stem.shape),
        final.mid.reshape(w_middle.shape),
        final.bot.reshape(w_bottom.shape),
        final.rise.reshape(3, 3, 3, f1, f2 + f1).transpose(0, 1, 2, 4, 3),
        final.fin.reshape(3, 3, 3, f0, f1 + f0).transpose(0, 1, 2, 4, 3),
        final.half.reshape(f0, w // 2, d // 2, h // 2),
    )


def solution(mesh):
    placed = (P("grp", "wid", "dep", "hgt"), P("grp", "wid", "dep", "hgt"), P(), P(), P(), P(), P())
    grad = P("grp", None, None, None, None)
    return jax.shard_map(
        local,
        mesh=mesh,
        in_specs=placed,
        out_specs=(P("grp", "wid", "dep", "hgt"), grad, grad, grad, grad, grad, P("grp", "wid", "dep", "hgt")),
        check_vma=False,
    )
```

time: 116 us -> 73.1 us (0.63)
  Pallas kernels: 94.1 us -> 72.1 us
  local copies, waits for them, and re-layouts: 21 us -> 0 us
    pallas_call x2, Pallas kernels: 94.1 us -> 72.1 us  [the longest x1 68.6 us: local(): pl.pallas_call(functools.partial(step_kernel, (f0, f1, f2, w, d, h), back...]
    unnamed x16 -> x0, local copies, waits for them, and re-layouts: 13 us -> none
    reshape x4 -> x0, local copies, waits for them, and re-layouts: 4.29 us -> none  [the longest x2 2.34 us: forward(): return v.reshape(-1, v.shape[4]).T]
    transpose x2 -> x0, local copies, waits for them, and re-layouts: 2.58 us -> none  [the longest x1 1.73 us: local(): cotangent.transpose(1, 2, 0, 3)]
where the time goes in v1:
time: 73.1 us; the launch traced here: 72.9 us
  Pallas kernels  72.1 us (99%)
  between operations  0.8 us (1%)
    pallas_call x1, Pallas kernels, local(): pl.pallas_call(functools.partial(step_kernel, (f0, f1, f2, w, d, h), back...  68.6 us
    pallas_call x1, Pallas kernels, local(): pl.pallas_call(functools.partial(unpack_kernel, (f0, f1, f2, h, scales),...  3.45 us

profile of v1, /device:TPU:0, one launch (start us, length us, event | category | flops | bytes accessed | tf_op | source)
XLA Modules:
  0.0 72.9 jit_solution(13738266641161878946)
XLA Ops:
  0.6 68.6 %unet_step.1 = (bf16[512,128]{1,0:T(8,128)(2,1)}, f32[128,128]{1,0:T(8,128)}, bf16[1024,128]{1,0:T(8,128)(2,1)}, bf16[1792,128]{1,0:T(8,128)(2,1)}, bf16[1792,12...) custom-call(bf16[512,128]{1,0:T(8,128)(2,1)} %bitcast.27, ...), custom_call_target="tpu_custom_call" | custom-call | tf_op jit(solution)/shard_map/unet_step/pallas_call | solution.py:776
  69.3 3.4 %unpack.1 = (bf16[512,128]{1,0:T(8,128)(2,1)}, f32[864,32]{1,0:T(8,128)}, f32[864,64]{1,0:T(8,128)}, f32[1728,128]{1,0:T(8,128)}, f32[27,64,192]{2,1,0:T(8,128)}...) custom-call(bf16[512,128]{1,0:T(8,128)(2,1)} %get-tuple-element.22.refs_0_, f32[128,128]{1,0:T(8,128)} %get-tuple-element.23.refs_1_, ...), custom_call_target="tpu_custom_call" | custom-call | tf_op jit(solution)/shard_map/unpack/pallas_call | solution.py:806

commit v2 on v1

--- a/solution.py
+++ b/solution.py
@@ -69,9 +69,18 @@
     return size
 
 
+def lane_parts(channels, tall, h, lanes):
+    count = lanes // h
+    while channels % (tall * count):
+        count -= 1
+    return count
+
+
 class Halo:
-    def __init__(self, group, rows, edges, own, span, sems):
+    def __init__(self, group, rows, packed, edges, own, span, sems):
         self.rows, self.edges, self.own = rows, edges, own
+        self.packed = packed
+        self.fold = rows.shape[2] // packed.shape[2]
         self.base = group * neighbours()
         self.w, self.d, self.h = span
         self.send, self.recv = sems
@@ -81,12 +90,16 @@
         self.tall = own.shape[0]
         self.per = rows.shape[2] // self.tall
 
+    def outer(self, a, b):
+        return a in (0, self.w + 1) or b in (0, self.d + 1)
+
     def clear(self):
-        blank = jnp.zeros(self.rows.shape[2:], BF)
+        moving = self.rows if self.fold == 1 else self.packed
+        blank = jnp.zeros(moving.shape[2:], BF)
         for a in range(self.w + 2):
             for b in range(self.d + 2):
-                if a in (0, self.w + 1) or b in (0, self.d + 1):
-                    self.rows[a, b] = blank
+                if self.outer(a, b):
+                    moving[a, b] = blank
         self.edges[...] = jnp.zeros(self.edges.shape, BF)
 
     def fill_edges(self):
@@ -102,7 +115,18 @@
                     tile = jnp.where(lane == self.side + r, part_of[:, self.h - 1 : self.h], tile)
         self.own[...] = tile.astype(BF)
 
+    def pack(self):
+        tall = self.packed.shape[2]
+        for a in range(1, self.w + 1):
+            for b in range(1, self.d + 1):
+                wide = self.rows[a, b].astype(F32)
+                total = wide[:tall]
+                for g in range(1, self.fold):
+                    total = total + pltpu.roll(wide[g * tall : (g + 1) * tall], g * self.h, 1)
+                self.packed[a, b] = total.astype(BF)
+
     def copies(self):
+        moving = self.rows if self.fold == 1 else self.packed
         place = {name: lax.axis_index(name) for name in AXES}
         size = {name: lax.axis_size(name) for name in AXES}
 
@@ -131,8 +155,8 @@
                     if ch == 0:
                         from_w, to_w = cells(sw, cw, self.w)
                         from_d, to_d = cells(sd, cd, self.d)
-                        source = self.rows.at[from_w, from_d]
-                        dest = self.rows.at[to_w, to_d]
+                        source = moving.at[from_w, from_d]
+                        dest = moving.at[to_w, to_d]
                     else:
                         source = self.own
                         dest = self.edges.at[(1 - sh) // 2, 1 - sw, 1 - sd]
@@ -158,6 +182,8 @@
         if self.before is not None:
             self.before.finish()
         self.fill_edges()
+        if self.fold > 1:
+            self.pack()
         for copy, can_send, _ in self.copies():
             self.guarded(can_send, copy.start)
         self.unsent = True
@@ -175,30 +201,39 @@
     def shifted(self, a, b, spread=None):
         lanes = self.own.shape[1]
         h = self.h if spread is None else 2 * self.h
-        row = self.rows[a, b]
+        folded = self.fold > 1 and self.outer(a, b)
+        tall = self.packed.shape[2] if folded else self.rows.shape[2]
+        row = self.packed[a, b] if folded else self.rows[a, b]
         if spread is not None:
-            row = mm(row, spread).astype(BF)
+            pieces = [mm(row, spread[g]) for g in range(self.fold if folded else 1)]
+            wide = pieces[0] if len(pieces) == 1 else jnp.concatenate(pieces, axis=0)
+            row = wide.astype(BF)
+            folded = False
+        else:
+            wide = row.astype(F32)
         dw = 0 if a == 0 else 2 if a == self.w + 1 else 1
         dd = 0 if b == 0 else 2 if b == self.d + 1 else 1
         r = ((self.w - 1, a - 1, 0)[dw] * self.d + (self.d - 1, b - 1, 0)[dd]) * self.per
-
         lane = lax.broadcasted_iota(jnp.int32, (self.tall, lanes), 1)
         low, high = self.edges[0, dw, dd].astype(F32), self.edges[1, dw, dd].astype(F32)
-        wide = row.astype(F32)
-        befores, afters = [], []
+        befores, centres, afters = [], [], []
         for g in range(self.per):
-            here = wide[g * self.tall : (g + 1) * self.tall]
+            turn, from_row = divmod(g * self.tall, tall) if folded else (0, g * self.tall)
+            here = wide[from_row : from_row + self.tall]
             left = low[:, self.side + r + g : self.side + r + g + 1]
             right = high[:, r + g : r + g + 1]
-            before = jnp.where(lane == 0, left, pltpu.roll(here, 1, 1))
-            after = jnp.where(lane == h - 1, right, pltpu.roll(here, lanes - 1, 1))
+            before = jnp.where(lane == 0, left, pltpu.roll(here, (lanes + 1 - turn * h) % lanes, 1))
+            after = jnp.where(lane == h - 1, right, pltpu.roll(here, lanes - 1 - turn * h, 1))
             if h < lanes:
                 before = jnp.where(lane < h, before, 0.0)
                 after = jnp.where(lane < h, after, 0.0)
             befores.append(before.astype(BF))
             afters.append(after.astype(BF))
-        if self.per == 1:
-            return befores[0], row, afters[0]
+            if folded:
+                centre = pltpu.roll(here, lanes - turn * h, 1) if turn else here
+                centres.append(jnp.where(lane < h, centre, 0.0).astype(BF))
+        if folded:
+            row = jnp.concatenate(centres, axis=0)
         return jnp.concatenate(befores, axis=0), row, jnp.concatenate(afters, axis=0)
 
 
@@ -313,7 +348,8 @@
         low=[(f1, blocks(27 * f1, lanes))],
         up=[(f1, blocks(27 * f2, lanes))],
         bot=[(27 * f1, blocks(f2, lanes))],
-        fin=[(3 * f0, blocks(9 * f1, lanes)), (3 * f0, blocks(9 * f0, lanes))],
+        early=[(3 * f0, blocks(9 * f0, lanes))],
+        fin=[(3 * f0, blocks(9 * f1, lanes))],
         mid=[(f1, blocks(27 * f0, lanes))],
         stem=[(f0, blocks(27 * f0, lanes))],
     )
@@ -324,8 +360,8 @@
 
 def orders():
     whole = math.prod(lax.axis_size(axis) for axis in GROUP)
-    near = (GROUP,) if whole <= 16 else STAGED
-    return dict(low=STAGED, up=STAGED, bot=STAGED, fin=STAGED, mid=near, stem=near)
+    near = (GROUP[:1], GROUP[1:]) if whole <= 16 else STAGED
+    return dict(low=STAGED, up=STAGED, bot=STAGED, early=STAGED, fin=STAGED, mid=STAGED, stem=near)
 
 
 def step_kernel(cfg, back, *refs):
@@ -337,7 +373,7 @@
     last = {}
     for name, (_, level, group) in HALOS.items():
         own = ref.halos[name]
-        halo[name] = Halo(group, own.rows, own.edges, own.own, spans[level], (ref.send, ref.recv))
+        halo[name] = Halo(group, own.rows, own.get(0, own.rows), own.edges, own.own, spans[level], (ref.send, ref.recv))
         halo[name].before = last.get(group)
         last[group] = halo[name]
     stacks = ref.stacks
@@ -350,8 +386,8 @@
     for i, name in enumerate(ref.ins):
         loads[name] = pltpu.make_async_copy(ref.ins[name], ref.inside[name], ref.load.at[i])
         loads[name].start()
-    for item in halo.values():
-        item.clear()
+    halo.feat.clear()
+    halo.cot.clear()
 
     def take(load, source, item):
         load.wait()
@@ -360,24 +396,32 @@
             for b in range(d):
                 item.rows[a + 1, b + 1] = ref.wide[pl.ds(a * d + b, f0, stride=w * d), :].astype(BF)
 
-    take(loads.feat, ref.inside.feat, halo.feat)
     barrier = pltpu.get_barrier_semaphore()
     me, everyone = position(GROUP)
     for k in range(1, everyone):
         pl.semaphore_signal(
             barrier, 1, device_id=device_at(GROUP, lax.rem(me + k, everyone)), device_id_type=pl.DeviceIdType.MESH
         )
+    take(loads.feat, ref.inside.feat, halo.feat)
+    halo.half.clear()
+    halo.stem.clear()
     pl.semaphore_wait(barrier, everyone - 1)
 
     halo.feat.start()
     take(loads.cot, ref.inside.cot, halo.cot)
     halo.cot.start()
+    for item in (halo.quarter, halo.deep, halo.rg, halo.dg, halo.mg, halo.mid, halo.ra):
+        item.clear()
     pool = pattern(lanes, lambda r, c: r // 2 == c)
     pool_mean = (pool / 8.0).astype(BF)
     pool_sum = pool.astype(BF)
     spread = pattern(lanes, lambda r, c: c // 2 == r)
     spread_mean = (spread / 8.0).astype(BF)
-    spread = spread.astype(BF)
+
+    def spreads(item):
+        full = 2 * item.h
+        each = [pattern(lanes, lambda r, c: (c < full) & (c // 2 == r - g * item.h)) for g in range(item.fold)]
+        return [v.astype(BF) for v in each]
 
     def forward(raw, target):
         target[...] = raw[...].reshape(-1, raw.shape[2]).T
@@ -411,9 +455,13 @@
                 target[a, b] = jnp.concatenate(parts[::-1] if back else parts, axis=0)
 
     def stack_up(up, target):
-        for a in range(target.shape[0]):
-            for b in range(target.shape[1]):
-                target[a, b] = jnp.concatenate(up.shifted((a + 1) // 2, (b + 1) // 2, spread), axis=0)
+        spread = spreads(up)
+        for i in range(up.w + 2):
+            for j in range(up.d + 2):
+                value = jnp.concatenate(up.shifted(i, j, spread), axis=0)
+                for a in range(max(2 * i - 1, 0), min(2 * i + 1, target.shape[0])):
+                    for b in range(max(2 * j - 1, 0), min(2 * j + 1, target.shape[1])):
+                        target[a, b] = value
 
     def patch(source, a, b, pair, back=False, middle=False):
         third = source.shape[2] // 3
@@ -512,7 +560,8 @@
     conv(stacks.stem, ref.w_fin_low, spans[0], final_low)
     cot_cells = lambda: beside(spans[0], lambda a, b: stacks.cot[a + 1, b + 1])
     low_cells = beside(spans[0], lambda a, b: patch(stacks.stem, a, b, 1, middle=True))
-    put_blocks(sums.fin.total, 3 * f0 * blocks(9 * f1, lanes), mm_nt(cot_cells(), low_cells))
+    put_blocks(sums.early.total, 0, mm_nt(cot_cells(), low_cells))
+    sums.early.step()
     halo.quarter.wait()
     stack(halo.quarter, stacks.quarter)
 
@@ -529,6 +578,7 @@
         ref.rise_pre[a, b] = value
 
     conv(stacks.mid, ref.w_rise_low, spans[1], rise_low)
+    sums.early.step()
     halo.deep.wait()
     stack_up(halo.deep, stacks.up2)
 
@@ -542,6 +592,7 @@
     halo.rg.start()
     halo.ra.start()
 
+    sums.early.step()
     grad1 = lambda item: beside(spans[1], lambda a, b: item.rows[a + 1, b + 1])
 
     def wide_wgrad(segment, grad, source, span):
@@ -572,6 +623,7 @@
             halo.dg.rows[a + 1, b + 1] = grad.astype(BF)
     halo.dg.start()
     sums.up.step()
+    sums.early.step()
     cells2 = beside(spans[2], lambda a, b: patch(stacks.quarter, a, b, 1))
     grad2 = beside(spans[2], lambda a, b: halo.dg.rows[a + 1, b + 1])
     bot = mm_nt(cells2, grad2)
@@ -583,6 +635,7 @@
     up_cells = beside(spans[0], lambda a, b: patch(stacks.up1, a, b, 1, middle=True))
     put_blocks(sums.fin.total, 0, mm_nt(cot_cells(), up_cells))
     sums.fin.step()
+    sums.bot.step()
     halo.dg.wait()
     stack(halo.dg, stacks.dg, back=True)
 
@@ -596,12 +649,19 @@
 
     conv(stacks.dg, ref.b_bot, spans[2], quarter_store, back=True)
     halo.mg.start()
+    sums.up.step()
+    sums.fin.step()
+    sums.early.step()
     wide_wgrad(sums.mid, grad1(halo.mg), stacks.half, spans[1])
     sums.mid.step()
-    sums.up.step()
-    sums.bot.step()
-    sums.fin.step()
+    def final_store(a, b, value):
+        ref.wide[pl.ds(a * d + b, f0, stride=w * d), :] = ref.fin_part[a, b] + value
+
+    conv(stacks.up1, ref.w_fin_up, spans[0], final_store)
+    ref.outs.output[...] = ref.wide[...].astype(BF)
     sums.low.step()
+    sums.mid.step()
+    sums.early.step()
     halo.mg.wait()
     stack(halo.mg, stacks.mg, back=True)
 
@@ -617,32 +677,35 @@
     conv(stacks.mg, ref.b_mid, spans[1], half_store, back=True)
     ref.outs.half[...] = ref.half_wide[...]
     wide_wgrad(sums.stem, beside(spans[0], lambda a, b: ref.stem_grad[a, b]), stacks.feat, spans[0])
+
     sums.stem.step()
-    sums.up.step()
     sums.bot.step()
     sums.fin.step()
+    sums.up.step()
+    sums.mid.step()
     sums.low.step()
-    sums.mid.step()
-
-    def final_store(a, b, value):
-        ref.wide[pl.ds(a * d + b, f0, stride=w * d), :] = ref.fin_part[a, b] + value
-
-    conv(stacks.up1, ref.w_fin_up, spans[0], final_store)
-    ref.outs.output[...] = ref.wide[...].astype(BF)
-    sums.stem.step()
-    sums.up.step()
-    sums.bot.step()
-    sums.fin.step()
-    sums.low.step()
-    sums.mid.step()
-    sums.up.step()
     sums.stem.step()
     sums.bot.step()
     sums.fin.step()
     sums.low.step()
     sums.up.step()
+    sums.mid.step()
+    sums.low.step()
+    sums.stem.step()
+    sums.bot.step()
+    sums.up.step()
+    sums.fin.step()
+    sums.mid.step()
+    sums.up.step()
+    sums.stem.step()
+    sums.stem.step()
     sums.bot.step()
     sums.fin.step()
+    sums.mid.step()
+    sums.bot.step()
+    sums.fin.step()
+    sums.mid.step()
+    sums.early.step()
     for item in sums.values():
         item.finish()
     for item in halo.values():
@@ -684,8 +747,9 @@
     ref.ready.bot[...] = side(ref.inside.bot, 0, 27 * f1, f2, scales.bot)[:, :f2]
     send(ref.ready.bot, ref.outs.bot)
     loads.fin.wait()
+    loads.early.wait()
     up = side(ref.inside.fin, 0, 3 * f0, 9 * f1, scales.fin)
-    low = side(ref.inside.fin, 3 * f0 * blocks(9 * f1, lanes), 3 * f0, 9 * f0, scales.fin)
+    low = side(ref.inside.early, 0, 3 * f0, 9 * f0, scales.fin)
     for k in range(27):
         at_, rows = k // 3, slice((k % 3) * f0, (k % 3 + 1) * f0)
         ref.ready.fin[k] = jnp.concatenate([up[rows, at_ * f1 : (at_ + 1) * f1], low[rows, at_ * f0 : (at_ + 1) * f0]], axis=1)
@@ -732,6 +796,9 @@
             edges=pltpu.VMEM((2, 3, 3, tall, h), BF),
             own=pltpu.VMEM((tall, h), BF),
         )
+        fold = lane_parts(f[c], tall, h >> level, h)
+        if fold > 1:
+            halos[name][0] = pltpu.VMEM((a + 2, b + 2, f[c] // fold, h), BF)
     place = segments(f, h)
     for name, order in orders().items():
         unit = TILE * math.prod(lax.axis_size(axis) for axis in GROUP)

time: 73.1 us -> 66 us (0.903)
  Pallas kernels: 72.1 us -> 65 us
    pallas_call x1, Pallas kernels: 68.6 us -> 61.6 us  [local(): pl.pallas_call(functools.partial(step_kernel, (f0, f1, f2, w, d, h), back...]
where the time goes in v2:
time: 66 us; the launch traced here: 65.8 us
  Pallas kernels  65 us (98%)
  between operations  0.8 us (1%)
    pallas_call x1, Pallas kernels, local(): pl.pallas_call(functools.partial(step_kernel, (f0, f1, f2, w, d, h), back...  61.6 us
    pallas_call x1, Pallas kernels, local(): pl.pallas_call(functools.partial(unpack_kernel, (f0, f1, f2, h, scales),...  3.46 us

profile of v2, /device:TPU:0, one launch (start us, length us, event | category | flops | bytes accessed | tf_op | source)
XLA Modules:
  0.0 65.8 jit_solution(11482857749569331884)
XLA Ops:
  0.6 61.6 %unet_step.1 = (bf16[512,128]{1,0:T(8,128)(2,1)}, f32[128,128]{1,0:T(8,128)}, bf16[1024,128]{1,0:T(8,128)(2,1)}, bf16[1792,128]{1,0:T(8,128)(2,1)}, bf16[1792,12...) custom-call(bf16[512,128]{1,0:T(8,128)(2,1)} %bitcast.27, ...), custom_call_target="tpu_custom_call" | custom-call | tf_op jit(solution)/shard_map/unet_step/pallas_call | solution.py:843
  62.2 3.5 %unpack.1 = (bf16[512,128]{1,0:T(8,128)(2,1)}, f32[864,32]{1,0:T(8,128)}, f32[864,64]{1,0:T(8,128)}, f32[1728,128]{1,0:T(8,128)}, f32[27,64,192]{2,1,0:T(8,128)}...) custom-call(bf16[512,128]{1,0:T(8,128)(2,1)} %get-tuple-element.23.refs_0_, f32[128,128]{1,0:T(8,128)} %get-tuple-element.24.refs_1_, ...), custom_call_target="tpu_custom_call" | custom-call | tf_op jit(solution)/shard_map/unpack/pallas_call | solution.py:873

commit v3 on v2

--- a/solution.py
+++ b/solution.py
@@ -81,7 +81,7 @@
         self.rows, self.edges, self.own = rows, edges, own
         self.packed = packed
         self.fold = rows.shape[2] // packed.shape[2]
-        self.base = group * neighbours()
+        self.base, self.sent_base = group * neighbours(), group // 2 * neighbours()
         self.w, self.d, self.h = span
         self.send, self.recv = sems
         self.before = None
@@ -163,12 +163,13 @@
                     copy = pltpu.make_async_remote_copy(
                         src_ref=source,
                         dst_ref=dest,
-                        send_sem=self.send.at[slot],
+                        send_sem=self.send.at[self.sent_base + len(out)],
                         recv_sem=self.recv.at[slot],
                         device_id=target,
                         device_id_type=pl.DeviceIdType.MESH,
                     )
-                    out.append((copy, [c for c in (ow, od, oh) if c is not True], [c for c in (iw, id_, ih) if c is not True]))
+                    steps = 2 * (cd > 0) + 2 * (ch > 0) + (cw > 0)
+                    out.append((copy, [c for c in (ow, od, oh) if c is not True], [c for c in (iw, id_, ih) if c is not True], steps))
         return out
 
     @staticmethod
@@ -184,17 +185,17 @@
         self.fill_edges()
         if self.fold > 1:
             self.pack()
-        for copy, can_send, _ in self.copies():
+        for copy, can_send, _, _ in sorted(self.copies(), key=lambda entry: -entry[3]):
             self.guarded(can_send, copy.start)
         self.unsent = True
 
     def wait(self):
-        for copy, _, can_take in self.copies():
+        for copy, _, can_take, _ in self.copies():
             self.guarded(can_take, copy.wait_recv)
 
     def finish(self):
         if self.unsent:
-            for copy, can_send, _ in self.copies():
+            for copy, can_send, _, _ in self.copies():
                 self.guarded(can_send, copy.wait_send)
         self.unsent = False
 
@@ -241,19 +242,35 @@
     return pl.ds(pl.multiple_of(i * m, TILE), m)
 
 
+def axis_part(axis):
+    return (axis, 1, lax.axis_size(axis)) if isinstance(axis, str) else axis
+
+
+def members(axes):
+    return math.prod(axis_part(axis)[2] for axis in axes)
+
+
 def position(axes):
     place, count = 0, 1
     for axis in axes:
-        place = place * lax.axis_size(axis) + lax.axis_index(axis)
-        count *= lax.axis_size(axis)
+        name, stride, n = axis_part(axis)
+        index = lax.axis_index(name)
+        if (stride, n) != (1, lax.axis_size(name)):
+            index = lax.rem(lax.div(index, stride), n)
+        place = place * n + index
+        count *= n
     return place, count
 
 
 def device_at(axes, place):
     where = {name: lax.axis_index(name) for name in GROUP}
     for axis in axes[::-1]:
-        n = lax.axis_size(axis)
-        where[axis] = place if axis == axes[0] else lax.rem(place, n)
+        name, stride, n = axis_part(axis)
+        to = place if axis == axes[0] else lax.rem(place, n)
+        if n == lax.axis_size(name):
+            where[name] = to
+        else:
+            where[name] = where[name] + (to - lax.rem(lax.div(where[name], stride), n)) * stride
         place = lax.div(place, n)
     return where
 
@@ -264,13 +281,13 @@
         self.levels = [buffers[3 * i : 3 * i + 3] for i in range(len(order))]
         self.total = buffers[0]
         self.send, self.recv = send, recv
-        self.stage, self.open, self.sent = 0, None, []
+        self.stage, self.open, self.last = 0, None, None
 
     def copy(self, stage, axes, source, dest, to):
         return pltpu.make_async_remote_copy(
             src_ref=source,
             dst_ref=dest,
-            send_sem=self.send.at[stage],
+            send_sem=self.send.at[0],
             recv_sem=self.recv.at[stage],
             device_id=device_at(axes, to),
             device_id_type=pl.DeviceIdType.MESH,
@@ -280,13 +297,19 @@
         i, n = position(axes)
         if n == 1:
             return
-        for k in range(1, n):
+        self.settle()
+        for k in sorted(range(1, n), key=lambda k: -min(k, n - k)):
             to = lax.rem(i + k, n)
             source, dest = pieces(to, i)
             self.copy(stage, axes, source, dest, to).start()
         every = whole.at[pl.ds(0, (n - 1) * m)]
         self.open = self.copy(stage, axes, every, every, lax.rem(i + 1, n))
-        self.sent.append(self.open)
+        self.last = self.open
+
+    def settle(self):
+        if self.last is not None:
+            self.last.wait_send()
+            self.last = None
 
     def step(self):
         stage, deep = self.stage, len(self.order)
@@ -324,13 +347,12 @@
     def finish(self):
         while self.stage <= 2 * len(self.order):
             self.step()
-        for copy in self.sent:
-            copy.wait_send()
+        self.settle()
 
 
 HALOS = dict(
     feat=(0, 0, 0), half=(0, 1, 1), quarter=(1, 2, 0), deep=(2, 2, 1), rg=(1, 1, 0), dg=(2, 2, 1),
-    mg=(1, 1, 0), cot=(0, 0, 2), mid=(1, 1, 2), stem=(0, 0, 3), ra=(1, 1, 3),
+    mg=(1, 1, 0), cot=(0, 0, 2), stem=(0, 0, 3), mid=(1, 1, 2), ra=(1, 1, 3),
 )
 STACKS = dict(
     feat=(0, 0), cot=(0, 0), half=(0, 1), quarter=(1, 2), up2=(2, 1), mid=(1, 1), up1=(1, 0),
@@ -342,11 +364,16 @@
     return -(-size // lanes)
 
 
+def split_at(count):
+    return count * 4 // 9
+
+
 def segments(f, lanes):
     f0, f1, f2 = f
     return dict(
         low=[(f1, blocks(27 * f1, lanes))],
-        up=[(f1, blocks(27 * f2, lanes))],
+        upa=[(f1, split_at(blocks(27 * f2, lanes)))],
+        upb=[(f1, blocks(27 * f2, lanes) - split_at(blocks(27 * f2, lanes)))],
         bot=[(27 * f1, blocks(f2, lanes))],
         early=[(3 * f0, blocks(9 * f0, lanes))],
         fin=[(3 * f0, blocks(9 * f1, lanes))],
@@ -359,9 +386,11 @@
 
 
 def orders():
-    whole = math.prod(lax.axis_size(axis) for axis in GROUP)
-    near = (GROUP[:1], GROUP[1:]) if whole <= 16 else STAGED
-    return dict(low=STAGED, up=STAGED, bot=STAGED, early=STAGED, fin=STAGED, mid=STAGED, stem=near)
+    near = (GROUP[:1], GROUP[1:]) if members(GROUP) <= 16 else STAGED
+    n = lax.axis_size("dep")
+    one, swap = ((GROUP,) if members(GROUP) <= 16 else STAGED), (STAGED[0], STAGED[2], STAGED[1])
+    pairs = (*STAGED[:2], (("dep", 1, 2),), (("dep", 2, n // 2),)) if n % 2 == 0 else STAGED
+    return dict(low=STAGED, upa=STAGED, upb=STAGED, bot=pairs, early=STAGED, fin=STAGED, mid=STAGED, stem=near)
 
 
 def step_kernel(cfg, back, *refs):
@@ -374,8 +403,8 @@
     for name, (_, level, group) in HALOS.items():
         own = ref.halos[name]
         halo[name] = Halo(group, own.rows, own.get(0, own.rows), own.edges, own.own, spans[level], (ref.send, ref.recv))
-        halo[name].before = last.get(group)
-        last[group] = halo[name]
+        halo[name].before = last.get(group // 2)
+        last[group // 2] = halo[name]
     stacks = ref.stacks
     sums = Names()
     for name, order in orders().items():
@@ -591,19 +620,23 @@
     conv(stacks.up2, ref.w_rise_up, spans[1], rise_store)
     halo.rg.start()
     halo.ra.start()
-
     sums.early.step()
+
     grad1 = lambda item: beside(spans[1], lambda a, b: item.rows[a + 1, b + 1])
 
-    def wide_wgrad(segment, grad, source, span):
-        cells = beside(span, lambda a, b: patch(source, a, b, 1))
+    def wide_wgrad(segment, grad, source, span, low=None, high=None):
+        cells = beside(span, lambda a, b: patch(source, a, b, 1)[low:high])
         put_blocks(segment.total, 0, mm_nt(grad, cells))
 
     wide_wgrad(sums.low, grad1(halo.rg), stacks.mid, spans[1])
     sums.low.step()
-    wide_wgrad(sums.up, grad1(halo.rg), stacks.up2, spans[1])
-    sums.up.step()
+    cut = split_at(blocks(27 * f2, lanes)) * lanes
+    wide_wgrad(sums.upa, grad1(halo.rg), stacks.up2, spans[1], None, cut)
+    sums.upa.step()
+    wide_wgrad(sums.upb, grad1(halo.rg), stacks.up2, spans[1], cut, None)
     sums.low.step()
+    sums.upb.step()
+    sums.upa.step()
     halo.rg.wait()
     stack(halo.rg, stacks.rg, back=True)
     deep_sum = [[None] * spans[2][1] for _ in range(spans[2][0])]
@@ -622,20 +655,21 @@
             grad = mm_split(deep_sum[a][b], pool_sum) * slope(ref.deep_pre[a, b])
             halo.dg.rows[a + 1, b + 1] = grad.astype(BF)
     halo.dg.start()
-    sums.up.step()
-    sums.early.step()
+    sums.upb.step()
     cells2 = beside(spans[2], lambda a, b: patch(stacks.quarter, a, b, 1))
     grad2 = beside(spans[2], lambda a, b: halo.dg.rows[a + 1, b + 1])
     bot = mm_nt(cells2, grad2)
     put_blocks(sums.bot.total, 0, bot)
     sums.bot.step()
+    sums.early.step()
     halo.ra.wait()
     stack_up(halo.ra, stacks.up1)
     sums.low.step()
+    sums.bot.step()
     up_cells = beside(spans[0], lambda a, b: patch(stacks.up1, a, b, 1, middle=True))
     put_blocks(sums.fin.total, 0, mm_nt(cot_cells(), up_cells))
+    sums.upa.step()
     sums.fin.step()
-    sums.bot.step()
     halo.dg.wait()
     stack(halo.dg, stacks.dg, back=True)
 
@@ -649,19 +683,28 @@
 
     conv(stacks.dg, ref.b_bot, spans[2], quarter_store, back=True)
     halo.mg.start()
-    sums.up.step()
     sums.fin.step()
-    sums.early.step()
+    sums.upb.step()
+
+    def final_row(a):
+        result = mm(ref.w_fin_up[...], patch(stacks.up1, a, 0, d))
+        for b in range(d):
+            value = ref.fin_part[a, b] + result[:, b * lanes : (b + 1) * lanes]
+            ref.wide[pl.ds(a * d + b, f0, stride=w * d), :] = value
+
     wide_wgrad(sums.mid, grad1(halo.mg), stacks.half, spans[1])
     sums.mid.step()
-    def final_store(a, b, value):
-        ref.wide[pl.ds(a * d + b, f0, stride=w * d), :] = ref.fin_part[a, b] + value
-
-    conv(stacks.up1, ref.w_fin_up, spans[0], final_store)
+    sums.low.step()
+    sums.early.step()
+    final_row(0)
+    final_row(1)
+    sums.upa.step()
+    sums.bot.step()
+    final_row(2)
+    sums.mid.step()
+    final_row(3)
     ref.outs.output[...] = ref.wide[...].astype(BF)
-    sums.low.step()
-    sums.mid.step()
-    sums.early.step()
+    sums.fin.step()
     halo.mg.wait()
     stack(halo.mg, stacks.mg, back=True)
 
@@ -676,36 +719,40 @@
 
     conv(stacks.mg, ref.b_mid, spans[1], half_store, back=True)
     ref.outs.half[...] = ref.half_wide[...]
+    sums.bot.step()
+    sums.low.step()
+    sums.upb.step()
     wide_wgrad(sums.stem, beside(spans[0], lambda a, b: ref.stem_grad[a, b]), stacks.feat, spans[0])
-
+    sums.stem.step()
+    sums.upa.step()
+
+    sums.mid.step()
+    sums.fin.step()
+    sums.stem.step()
+    sums.low.step()
+    sums.early.step()
+    sums.upb.step()
+    sums.bot.step()
+    sums.upa.step()
+    sums.fin.step()
+    sums.mid.step()
     sums.stem.step()
     sums.bot.step()
-    sums.fin.step()
-    sums.up.step()
-    sums.mid.step()
     sums.low.step()
-    sums.stem.step()
-    sums.bot.step()
-    sums.fin.step()
-    sums.low.step()
-    sums.up.step()
-    sums.mid.step()
-    sums.low.step()
-    sums.stem.step()
-    sums.bot.step()
-    sums.up.step()
-    sums.fin.step()
-    sums.mid.step()
-    sums.up.step()
-    sums.stem.step()
+    sums.upa.step()
+    sums.upb.step()
     sums.stem.step()
     sums.bot.step()
     sums.fin.step()
     sums.mid.step()
+    sums.upb.step()
+    sums.stem.step()
     sums.bot.step()
+    sums.mid.step()
     sums.fin.step()
+    sums.early.step()
+    sums.bot.step()
     sums.mid.step()
-    sums.early.step()
     for item in sums.values():
         item.finish()
     for item in halo.values():
@@ -715,10 +762,6 @@
 def unpack_kernel(cfg, back, *refs):
     (f0, f1, f2, lanes, scales) = cfg
     ref = back(iter(refs))
-    loads = Names()
-    for i, name in enumerate(ref.ins):
-        loads[name] = pltpu.make_async_copy(ref.ins[name], ref.inside[name], ref.load.at[i])
-        loads[name].start()
     stores = []
 
     def send(source, target):
@@ -731,34 +774,29 @@
         value = [source[base + j * rows : base + (j + 1) * rows].astype(F32) * scale for j in range(count)]
         return jnp.concatenate(value, axis=1)
 
-    loads.output.wait()
-    send(ref.inside.output, ref.outs.output)
-    loads.half.wait()
-    ref.ready.half[...] = ref.inside.half[:, : lanes // 2]
+    send(ref.ins.output, ref.outs.output)
+    ref.ready.half[...] = ref.ins.half[:, : lanes // 2]
     send(ref.ready.half, ref.outs.half)
-    loads.low.wait()
-    loads.up.wait()
-    low = side(ref.inside.low, 0, f1, 27 * f1, scales.rise)
-    up = side(ref.inside.up, 0, f1, 27 * f2, scales.rise)
+    ref.ready.bot[...] = side(ref.ins.bot, 0, 27 * f1, f2, scales.bot)[:, :f2]
+    send(ref.ready.bot, ref.outs.bot)
+    low = side(ref.ins.low, 0, f1, 27 * f1, scales.rise)
+    first = split_at(blocks(27 * f2, lanes))
+    up = [side(ref.ins.upa, 0, f1, first * lanes, scales.rise)]
+    up.append(side(ref.ins.upb, 0, f1, 27 * f2 - first * lanes, scales.rise))
+    up = jnp.concatenate(up, axis=1)
     for k in range(27):
         ref.ready.rise[k] = jnp.concatenate([up[:, k * f2 : (k + 1) * f2], low[:, k * f1 : (k + 1) * f1]], axis=1)
     send(ref.ready.rise, ref.outs.rise)
-    loads.bot.wait()
-    ref.ready.bot[...] = side(ref.inside.bot, 0, 27 * f1, f2, scales.bot)[:, :f2]
-    send(ref.ready.bot, ref.outs.bot)
-    loads.fin.wait()
-    loads.early.wait()
-    up = side(ref.inside.fin, 0, 3 * f0, 9 * f1, scales.fin)
-    low = side(ref.inside.early, 0, 3 * f0, 9 * f0, scales.fin)
+    up = side(ref.ins.fin, 0, 3 * f0, 9 * f1, scales.fin)
+    low = side(ref.ins.early, 0, 3 * f0, 9 * f0, scales.fin)
     for k in range(27):
         at_, rows = k // 3, slice((k % 3) * f0, (k % 3 + 1) * f0)
         ref.ready.fin[k] = jnp.concatenate([up[rows, at_ * f1 : (at_ + 1) * f1], low[rows, at_ * f0 : (at_ + 1) * f0]], axis=1)
     send(ref.ready.fin, ref.outs.fin)
-    for load, source, target, out, scale in (
-        (loads.mid, ref.inside.mid, ref.ready.mid, ref.outs.mid, scales.mid),
-        (loads.stem, ref.inside.stem, ref.ready.stem, ref.outs.stem, scales.stem),
+    for source, target, out, scale in (
+        (ref.ins.mid, ref.ready.mid, ref.outs.mid, scales.mid),
+        (ref.ins.stem, ref.ready.stem, ref.outs.stem, scales.stem),
     ):
-        load.wait()
         width = target.shape[1]
         for j in range(blocks(27 * f0, lanes)):
             value = (source[j * width : (j + 1) * width].astype(F32) * scale).T
@@ -801,16 +839,15 @@
             halos[name][0] = pltpu.VMEM((a + 2, b + 2, f[c] // fold, h), BF)
     place = segments(f, h)
     for name, order in orders().items():
-        unit = TILE * math.prod(lax.axis_size(axis) for axis in GROUP)
+        unit = TILE * members(GROUP)
         rows = -(-sum(a * b for a, b in place[name]) // unit) * unit
         outs[name] = jax.ShapeDtypeStruct((rows, h), BF)
         levels = {}
         for i, axes in enumerate(order):
             for j, kind in enumerate((F32, BF, BF)):
                 levels[3 * i + j] = pltpu.VMEM((rows, h), kind)
-            rows //= math.prod(lax.axis_size(axis) for axis in axes)
-        several = pltpu.SemaphoreType.DMA((2 * len(order),))
-        sums[name] = dict(levels=levels, send=several, recv=several)
+            rows //= members(axes)
+        sums[name] = dict(levels=levels, send=pltpu.SemaphoreType.DMA((1,)), recv=pltpu.SemaphoreType.DMA((2 * len(order),)))
 
     def cells_of(c, level, kind=F32):
         return pltpu.VMEM((*spans[level], c, h), kind)
@@ -819,7 +856,7 @@
         return pltpu.VMEM((a, 27 * b), BF)
 
     scratch = dict(
-        send=pltpu.SemaphoreType.DMA((sets * near,)),
+        send=pltpu.SemaphoreType.DMA((blocks(sets, 2) * near,)),
         recv=pltpu.SemaphoreType.DMA((sets * near,)),
         load=pltpu.SemaphoreType.DMA((len(inputs),)),
         inside={name: pltpu.VMEM(v.shape, BF) for name, v in inputs.items()},
@@ -846,11 +883,11 @@
         in_specs=[anywhere] * len(inputs),
         out_specs=(vmem,) * len(outs),
         scratch_shapes=leaves[len(inputs) + len(outs) :],
-        compiler_params=pltpu.CompilerParams(collective_id=0, has_side_effects=True, vmem_limit_bytes=60 << 20),
+        compiler_params=pltpu.CompilerParams(collective_id=0, has_side_effects=True, vmem_limit_bytes=52 << 20),
         name="unet_step",
-    )(*inputs.values())
+    )(*[pltpu.with_memory_space_constraint(v, pltpu.HBM) for v in inputs.values()])
     packed = dict(zip(outs, done))
-    cells = w * d * h * math.prod(lax.axis_size(axis) for axis in GROUP)
+    cells = w * d * h * members(GROUP)
     fine, mid, deep = (1.0 / math.sqrt(cells / k) for k in (1.0, 8.0, 64.0))
     scales = Names(stem=fine, mid=mid, bot=deep, rise=mid, fin=fine)
 
@@ -864,19 +901,17 @@
         half=jax.ShapeDtypeStruct((flat // 4, h // 2), F32),
     )
     hold = dict(
-        inside={n: pltpu.VMEM(v.shape, v.dtype) for n, v in packed.items()},
         ready={n: pltpu.VMEM(v.shape, v.dtype) for n, v in results.items()},
-        load=pltpu.SemaphoreType.DMA((len(packed),)),
         store=pltpu.SemaphoreType.DMA((len(results),)),
     )
     leaves, back = spread_out(dict(ins=packed, outs=results, **hold))
     final = pl.pallas_call(
         functools.partial(unpack_kernel, (f0, f1, f2, h, scales), back),
         out_shape=tuple(results.values()),
-        in_specs=[anywhere] * len(packed),
+        in_specs=[vmem] * len(packed),
         out_specs=(anywhere,) * len(results),
         scratch_shapes=leaves[len(packed) + len(results) :],
-        compiler_params=pltpu.CompilerParams(vmem_limit_bytes=60 << 20),
+        compiler_params=pltpu.CompilerParams(vmem_limit_bytes=46 << 20),
         name="unpack",
     )(*packed.values())
     final = Names(zip(results, final))

time: 66 us -> 61 us (0.924)
  Pallas kernels: 65 us -> 60.1 us
    pallas_call x1, Pallas kernels: 61.6 us -> 57.5 us  [local(): pl.pallas_call(functools.partial(step_kernel, (f0, f1, f2, w, d, h), back...]
    pallas_call x1, Pallas kernels: 3.46 us -> 2.6 us  [local(): pl.pallas_call(functools.partial(unpack_kernel, (f0, f1, f2, h, scales),...]
where the time goes in v3:
time: 61 us; the launch traced here: 60.9 us
  Pallas kernels  60.1 us (99%)
  between operations  0.8 us (1%)
    pallas_call x1, Pallas kernels, local(): pl.pallas_call(functools.partial(step_kernel, (f0, f1, f2, w, d, h), back...  57.5 us
    pallas_call x1, Pallas kernels, local(): pl.pallas_call(functools.partial(unpack_kernel, (f0, f1, f2, h, scales),...  2.6 us

profile of v3, /device:TPU:0, one launch (start us, length us, event | category | flops | bytes accessed | tf_op | source)
XLA Modules:
  0.0 60.9 jit_solution(7683859327536269098)
XLA Ops:
  0.6 57.5 %unet_step.1 = (bf16[512,128]{1,0:T(8,128)(2,1)S(1)}, f32[128,128]{1,0:T(8,128)S(1)}, bf16[1024,128]{1,0:T(8,128)(2,1)S(1)}, bf16[768,128]{1,0:T(8,128)(2,1)S(1)...) custom-call(bf16[512,128]{1,0:T(8,128)(2,1)} %bitcast.27, ...), custom_call_target="tpu_custom_call" | custom-call | tf_op jit(solution)/shard_map/unet_step/pallas_call | solution.py:880
  58.1 2.6 %unpack.1 = (bf16[512,128]{1,0:T(8,128)(2,1)}, f32[864,32]{1,0:T(8,128)}, f32[864,64]{1,0:T(8,128)}, f32[1728,128]{1,0:T(8,128)}, f32[27,64,192]{2,1,0:T(8,128)}...) custom-call(bf16[512,128]{1,0:T(8,128)(2,1)S(1)} %get-tuple-element.24.refs_0_, f32[128,128]{1,0:T(8,128)S(1)} %get-tuple-element.25.refs_1_, ...), custom_call_target="tpu_custom_call" | custom-call | tf_op jit(solution)/shard_map/unpack/pallas_call | solution.py:908

commit v4 on v3

--- a/solution.py
+++ b/solution.py
@@ -374,7 +374,8 @@
         low=[(f1, blocks(27 * f1, lanes))],
         upa=[(f1, split_at(blocks(27 * f2, lanes)))],
         upb=[(f1, blocks(27 * f2, lanes) - split_at(blocks(27 * f2, lanes)))],
-        bot=[(27 * f1, blocks(f2, lanes))],
+        bota=[(16 * f1, blocks(f2, lanes))],
+        botb=[(11 * f1, blocks(f2, lanes))],
         early=[(3 * f0, blocks(9 * f0, lanes))],
         fin=[(3 * f0, blocks(9 * f1, lanes))],
         mid=[(f1, blocks(27 * f0, lanes))],
@@ -390,7 +391,7 @@
     n = lax.axis_size("dep")
     one, swap = ((GROUP,) if members(GROUP) <= 16 else STAGED), (STAGED[0], STAGED[2], STAGED[1])
     pairs = (*STAGED[:2], (("dep", 1, 2),), (("dep", 2, n // 2),)) if n % 2 == 0 else STAGED
-    return dict(low=STAGED, upa=STAGED, upb=STAGED, bot=pairs, early=STAGED, fin=STAGED, mid=STAGED, stem=near)
+    return dict(low=STAGED, upa=STAGED, upb=STAGED, bota=pairs, botb=pairs, early=STAGED, fin=STAGED, mid=STAGED, stem=near)
 
 
 def step_kernel(cfg, back, *refs):
@@ -608,6 +609,10 @@
 
     conv(stacks.mid, ref.w_rise_low, spans[1], rise_low)
     sums.early.step()
+    for held in (ref.stem_pre, ref.mid_pre, ref.deep_pre):
+        for a in range(held.shape[0]):
+            for b in range(held.shape[1]):
+                held[a, b] = slope(held[a, b])
     halo.deep.wait()
     stack_up(halo.deep, stacks.up2)
 
@@ -652,22 +657,25 @@
                 deep_sum[ap][bt] = value[:f2] if old is None else old + value[:f2]
     for a in range(spans[2][0]):
         for b in range(spans[2][1]):
-            grad = mm_split(deep_sum[a][b], pool_sum) * slope(ref.deep_pre[a, b])
+            grad = mm_split(deep_sum[a][b], pool_sum) * ref.deep_pre[a, b]
             halo.dg.rows[a + 1, b + 1] = grad.astype(BF)
     halo.dg.start()
     sums.upb.step()
     cells2 = beside(spans[2], lambda a, b: patch(stacks.quarter, a, b, 1))
     grad2 = beside(spans[2], lambda a, b: halo.dg.rows[a + 1, b + 1])
     bot = mm_nt(cells2, grad2)
-    put_blocks(sums.bot.total, 0, bot)
-    sums.bot.step()
+    put_blocks(sums.bota.total, 0, bot[: 16 * f1])
+    put_blocks(sums.botb.total, 0, bot[16 * f1 :])
+    sums.bota.step()
+    sums.botb.step()
     sums.early.step()
     halo.ra.wait()
     stack_up(halo.ra, stacks.up1)
     sums.low.step()
-    sums.bot.step()
     up_cells = beside(spans[0], lambda a, b: patch(stacks.up1, a, b, 1, middle=True))
     put_blocks(sums.fin.total, 0, mm_nt(cot_cells(), up_cells))
+    sums.bota.step()
+    sums.botb.step()
     sums.upa.step()
     sums.fin.step()
     halo.dg.wait()
@@ -678,7 +686,7 @@
         for i in range(2):
             for j in range(2):
                 at_, bt = 2 * a + i, 2 * b + j
-                grad = (ref.rb_skip[at_, bt] + wide) * slope(ref.mid_pre[at_, bt])
+                grad = (ref.rb_skip[at_, bt] + wide) * ref.mid_pre[at_, bt]
                 halo.mg.rows[at_ + 1, bt + 1] = grad.astype(BF)
 
     conv(stacks.dg, ref.b_bot, spans[2], quarter_store, back=True)
@@ -696,10 +704,11 @@
     sums.mid.step()
     sums.low.step()
     sums.early.step()
+    sums.bota.step()
     final_row(0)
     final_row(1)
+    sums.botb.step()
     sums.upa.step()
-    sums.bot.step()
     final_row(2)
     sums.mid.step()
     final_row(3)
@@ -714,45 +723,51 @@
         for i in range(2):
             for j in range(2):
                 at_, bt = 2 * a + i, 2 * b + j
-                grad = (ref.fb_skip[at_, bt] + wide) * slope(ref.stem_pre[at_, bt])
+                grad = (ref.fb_skip[at_, bt] + wide) * ref.stem_pre[at_, bt]
                 ref.stem_grad[at_, bt] = grad.astype(BF)
 
     conv(stacks.mg, ref.b_mid, spans[1], half_store, back=True)
     ref.outs.half[...] = ref.half_wide[...]
-    sums.bot.step()
     sums.low.step()
+    sums.bota.step()
     sums.upb.step()
     wide_wgrad(sums.stem, beside(spans[0], lambda a, b: ref.stem_grad[a, b]), stacks.feat, spans[0])
     sums.stem.step()
+    sums.botb.step()
     sums.upa.step()
 
     sums.mid.step()
     sums.fin.step()
     sums.stem.step()
+    sums.bota.step()
     sums.low.step()
     sums.early.step()
     sums.upb.step()
-    sums.bot.step()
+    sums.botb.step()
     sums.upa.step()
+    sums.mid.step()
     sums.fin.step()
-    sums.mid.step()
-    sums.stem.step()
-    sums.bot.step()
+    sums.bota.step()
     sums.low.step()
     sums.upa.step()
     sums.upb.step()
+    sums.botb.step()
     sums.stem.step()
-    sums.bot.step()
-    sums.fin.step()
-    sums.mid.step()
-    sums.upb.step()
-    sums.stem.step()
-    sums.bot.step()
     sums.mid.step()
     sums.fin.step()
+    sums.bota.step()
+    sums.upb.step()
+    sums.botb.step()
+    sums.stem.step()
+    sums.mid.step()
+    sums.bota.step()
+    sums.fin.step()
     sums.early.step()
-    sums.bot.step()
+    sums.stem.step()
+    sums.botb.step()
+    sums.bota.step()
     sums.mid.step()
+    sums.botb.step()
     for item in sums.values():
         item.finish()
     for item in halo.values():
@@ -777,7 +792,8 @@
     send(ref.ins.output, ref.outs.output)
     ref.ready.half[...] = ref.ins.half[:, : lanes // 2]
     send(ref.ready.half, ref.outs.half)
-    ref.ready.bot[...] = side(ref.ins.bot, 0, 27 * f1, f2, scales.bot)[:, :f2]
+    ref.ready.bot[: 16 * f1] = side(ref.ins.bota, 0, 16 * f1, f2, scales.bot)[:, :f2]
+    ref.ready.bot[16 * f1 :] = side(ref.ins.botb, 0, 11 * f1, f2, scales.bot)[:, :f2]
     send(ref.ready.bot, ref.outs.bot)
     low = side(ref.ins.low, 0, f1, 27 * f1, scales.rise)
     first = split_at(blocks(27 * f2, lanes))
@@ -883,7 +899,7 @@
         in_specs=[anywhere] * len(inputs),
         out_specs=(vmem,) * len(outs),
         scratch_shapes=leaves[len(inputs) + len(outs) :],
-        compiler_params=pltpu.CompilerParams(collective_id=0, has_side_effects=True, vmem_limit_bytes=52 << 20),
+        compiler_params=pltpu.CompilerParams(collective_id=0, has_side_effects=True, vmem_limit_bytes=58 << 20),
         name="unet_step",
     )(*[pltpu.with_memory_space_constraint(v, pltpu.HBM) for v in inputs.values()])
     packed = dict(zip(outs, done))

time: 61 us -> 70.1 us (1.15)
  local copies, waits for them, and re-layouts: 0 us -> 9.99 us
  Pallas kernels: 60.1 us -> 58.9 us
    unnamed x0 -> x22, local copies, waits for them, and re-layouts: none -> 9.99 us
    pallas_call x1, Pallas kernels: 57.5 us -> 56.3 us  [local(): pl.pallas_call(functools.partial(step_kernel, (f0, f1, f2, w, d, h), back...]
where the time goes in v4:
time: 70.1 us; the launch traced here: 69.7 us
  Pallas kernels  58.9 us (84%)
  local copies, waits for them, and re-layouts  9.99 us (14%)
  between operations  0.82 us (1%)
    pallas_call x1, Pallas kernels, local(): pl.pallas_call(functools.partial(step_kernel, (f0, f1, f2, w, d, h), back...  56.3 us
    unnamed x22, local copies, waits for them, and re-layouts  9.99 us
    pallas_call x1, Pallas kernels, local(): pl.pallas_call(functools.partial(unpack_kernel, (f0, f1, f2, h, scales),...  2.57 us

profile of v4, /device:TPU:0, one launch (start us, length us, event | category | flops | bytes accessed | tf_op | source)
XLA Modules:
  0.0 69.7 jit_solution(2296979355044168363)
XLA Ops:
  0.6 56.3 %unet_step.1 = (bf16[512,128]{1,0:T(8,128)(2,1)}, f32[128,128]{1,0:T(8,128)}, bf16[1024,128]{1,0:T(8,128)(2,1)}, bf16[768,128]{1,0:T(8,128)(2,1)}, bf16[1024,128...) custom-call(bf16[512,128]{1,0:T(8,128)(2,1)} %bitcast.27, ...), custom_call_target="tpu_custom_call" | custom-call | tf_op jit(solution)/shard_map/unet_step/pallas_call | solution.py:896
  57.0 0.0 copy-start
  57.0 0.9 %copy-done = bf16[1024,128]{1,0:T(8,128)(2,1)S(1)} copy-done((bf16[1024,128]{1,0:T(8,128)(2,1)S(1)}, bf16[1024,128]{1,0:T(8,128)(2,1)}, u32[]{:S(2)}) %copy-start) | copy-done | bytes 262168
  57.9 0.0 copy-start.1
  57.9 0.9 %copy-done.1 = bf16[1024,128]{1,0:T(8,128)(2,1)S(1)} copy-done((bf16[1024,128]{1,0:T(8,128)(2,1)S(1)}, bf16[1024,128]{1,0:T(8,128)(2,1)}, u32[]{:S(2)}) %copy-start.1) | copy-done | bytes 262168
  58.9 0.0 copy-start.2
  58.9 0.9 %copy-done.2 = bf16[1024,128]{1,0:T(8,128)(2,1)S(1)} copy-done((bf16[1024,128]{1,0:T(8,128)(2,1)S(1)}, bf16[1024,128]{1,0:T(8,128)(2,1)}, u32[]{:S(2)}) %copy-start.2) | copy-done | bytes 262168
  59.8 0.0 copy-start.3
  59.8 0.9 %copy-done.3 = bf16[768,128]{1,0:T(8,128)(2,1)S(1)} copy-done((bf16[768,128]{1,0:T(8,128)(2,1)S(1)}, bf16[768,128]{1,0:T(8,128)(2,1)}, u32[]{:S(2)}) %copy-start.3) | copy-done | bytes 196632
  60.7 0.0 copy-start.4
  60.7 0.9 %copy-done.4 = bf16[768,128]{1,0:T(8,128)(2,1)S(1)} copy-done((bf16[768,128]{1,0:T(8,128)(2,1)S(1)}, bf16[768,128]{1,0:T(8,128)(2,1)}, u32[]{:S(2)}) %copy-start.4) | copy-done | bytes 196632
  61.7 0.0 copy-start.5
  61.7 0.9 %copy-done.5 = bf16[512,128]{1,0:T(8,128)(2,1)S(1)} copy-done((bf16[512,128]{1,0:T(8,128)(2,1)S(1)}, bf16[512,128]{1,0:T(8,128)(2,1)}, u32[]{:S(2)}) %copy-start.5) | copy-done | bytes 131096
  62.6 0.0 copy-start.6
  62.6 0.9 %copy-done.6 = bf16[512,128]{1,0:T(8,128)(2,1)S(1)} copy-done((bf16[512,128]{1,0:T(8,128)(2,1)S(1)}, bf16[512,128]{1,0:T(8,128)(2,1)}, u32[]{:S(2)}) %copy-start.6) | copy-done | bytes 131096
  63.5 0.0 copy-start.7
  63.5 0.9 %copy-done.7 = bf16[512,128]{1,0:T(8,128)(2,1)S(1)} copy-done((bf16[512,128]{1,0:T(8,128)(2,1)S(1)}, bf16[512,128]{1,0:T(8,128)(2,1)}, u32[]{:S(2)}) %copy-start.7) | copy-done | bytes 131096
  64.4 0.0 copy-start.8
  64.4 0.9 %copy-done.8 = bf16[512,128]{1,0:T(8,128)(2,1)S(1)} copy-done((bf16[512,128]{1,0:T(8,128)(2,1)S(1)}, bf16[512,128]{1,0:T(8,128)(2,1)}, u32[]{:S(2)}) %copy-start.8) | copy-done | bytes 131096
  65.3 0.0 copy-start.9
  65.3 0.8 %copy-done.9 = f32[128,128]{1,0:T(8,128)S(1)} copy-done((f32[128,128]{1,0:T(8,128)S(1)}, f32[128,128]{1,0:T(8,128)}, u32[]{:S(2)}) %copy-start.9) | copy-done | bytes 65560
  66.1 0.0 copy-start.10
  66.1 0.8 %copy-done.10 = bf16[256,128]{1,0:T(8,128)(2,1)S(1)} copy-done((bf16[256,128]{1,0:T(8,128)(2,1)S(1)}, bf16[256,128]{1,0:T(8,128)(2,1)}, u32[]{:S(2)}) %copy-start.10) | copy-done | bytes 65560
  67.0 2.6 %unpack.1 = (bf16[512,128]{1,0:T(8,128)(2,1)}, f32[864,32]{1,0:T(8,128)}, f32[864,64]{1,0:T(8,128)}, f32[1728,128]{1,0:T(8,128)}, f32[27,64,192]{2,1,0:T(8,128)}...) custom-call(bf16[512,128]{1,0:T(8,128)(2,1)S(1)} %copy-done.5, f32[128,128]{1,0:T(8,128)S(1)} %copy-done.9, ...), custom_call_target="tpu_custom_call" | custom-call | tf_op jit(solution)/shard_map/unpack/pallas_call | solution.py:924
Async XLA Ops:
  57.0 1.0 %copy-start = (bf16[1024,128]{1,0:T(8,128)(2,1)S(1)}, bf16[1024,128]{1,0:T(8,128)(2,1)}, u32[]{:S(2)}) copy-start(bf16[1024,128]{1,0:T(8,128)(2,1)} %get-tuple-element.27.refs_2_) | copy-start | bytes 786436
  57.9 0.9 %copy-start.1 = (bf16[1024,128]{1,0:T(8,128)(2,1)S(1)}, bf16[1024,128]{1,0:T(8,128)(2,1)}, u32[]{:S(2)}) copy-start(bf16[1024,128]{1,0:T(8,128)(2,1)} %get-tuple-element.29.refs_4_) | copy-start | bytes 786436
  58.9 0.9 %copy-start.2 = (bf16[1024,128]{1,0:T(8,128)(2,1)S(1)}, bf16[1024,128]{1,0:T(8,128)(2,1)}, u32[]{:S(2)}) copy-start(bf16[1024,128]{1,0:T(8,128)(2,1)} %get-tuple-element.30.refs_5_) | copy-start | bytes 786436
  59.8 0.9 %copy-start.3 = (bf16[768,128]{1,0:T(8,128)(2,1)S(1)}, bf16[768,128]{1,0:T(8,128)(2,1)}, u32[]{:S(2)}) copy-start(bf16[768,128]{1,0:T(8,128)(2,1)} %get-tuple-element.28.refs_3_) | copy-start | bytes 589828
  60.7 0.9 %copy-start.4 = (bf16[768,128]{1,0:T(8,128)(2,1)S(1)}, bf16[768,128]{1,0:T(8,128)(2,1)}, u32[]{:S(2)}) copy-start(bf16[768,128]{1,0:T(8,128)(2,1)} %get-tuple-element.31.refs_6_) | copy-start | bytes 589828
  61.7 0.9 %copy-start.5 = (bf16[512,128]{1,0:T(8,128)(2,1)S(1)}, bf16[512,128]{1,0:T(8,128)(2,1)}, u32[]{:S(2)}) copy-start(bf16[512,128]{1,0:T(8,128)(2,1)} %get-tuple-element.25.refs_0_) | copy-start | bytes 393220
  62.6 0.9 %copy-start.6 = (bf16[512,128]{1,0:T(8,128)(2,1)S(1)}, bf16[512,128]{1,0:T(8,128)(2,1)}, u32[]{:S(2)}) copy-start(bf16[512,128]{1,0:T(8,128)(2,1)} %get-tuple-element.32.refs_7_) | copy-start | bytes 393220
  63.5 0.9 %copy-start.7 = (bf16[512,128]{1,0:T(8,128)(2,1)S(1)}, bf16[512,128]{1,0:T(8,128)(2,1)}, u32[]{:S(2)}) copy-start(bf16[512,128]{1,0:T(8,128)(2,1)} %get-tuple-element.33.refs_8_) | copy-start | bytes 393220
  64.4 0.9 %copy-start.8 = (bf16[512,128]{1,0:T(8,128)(2,1)S(1)}, bf16[512,128]{1,0:T(8,128)(2,1)}, u32[]{:S(2)}) copy-start(bf16[512,128]{1,0:T(8,128)(2,1)} %get-tuple-element.34.refs_9_) | copy-start | bytes 393220
  65.3 0.8 %copy-start.9 = (f32[128,128]{1,0:T(8,128)S(1)}, f32[128,128]{1,0:T(8,128)}, u32[]{:S(2)}) copy-start(f32[128,128]{1,0:T(8,128)} %get-tuple-element.26.refs_1_) | copy-start | bytes 196612
  66.1 0.8 %copy-start.10 = (bf16[256,128]{1,0:T(8,128)(2,1)S(1)}, bf16[256,128]{1,0:T(8,128)(2,1)}, u32[]{:S(2)}) copy-start(bf16[256,128]{1,0:T(8,128)(2,1)} %get-tuple-element.35.refs_10_) | copy-start | bytes 196612

commit v5 on v4

--- a/solution.py
+++ b/solution.py
@@ -890,6 +890,7 @@
         w_fin_up=taps(f0, f1), w_fin_low=taps(f0, f0), b_mid=taps(f0, f1), b_bot=taps(f1, f2),
         b_rise=taps(f2 + f1, f1), b_fin=taps(f1 + f0, f0),
     )
+    grant = 46 if members(GROUP) <= 16 else 60
     vmem = pl.BlockSpec(memory_space=pltpu.VMEM)
     anywhere = pl.BlockSpec(memory_space=pl.ANY)
     leaves, back = spread_out(dict(ins=inputs, outs=outs, **scratch))
@@ -899,7 +900,7 @@
         in_specs=[anywhere] * len(inputs),
         out_specs=(vmem,) * len(outs),
         scratch_shapes=leaves[len(inputs) + len(outs) :],
-        compiler_params=pltpu.CompilerParams(collective_id=0, has_side_effects=True, vmem_limit_bytes=58 << 20),
+        compiler_params=pltpu.CompilerParams(collective_id=0, has_side_effects=True, vmem_limit_bytes=grant << 20),
         name="unet_step",
     )(*[pltpu.with_memory_space_constraint(v, pltpu.HBM) for v in inputs.values()])
     packed = dict(zip(outs, done))

time: 70.1 us -> 58.6 us (0.84)
  local copies, waits for them, and re-layouts: 9.99 us -> 0 us
  Pallas kernels: 58.9 us -> 57.6 us
    unnamed x22 -> x0, local copies, waits for them, and re-layouts: 9.99 us -> none
    pallas_call x1, Pallas kernels: 56.3 us -> 55 us  [local(): pl.pallas_call(functools.partial(step_kernel, (f0, f1, f2, w, d, h), back...]
where the time goes in v5:
time: 58.6 us; the launch traced here: 58.4 us
  Pallas kernels  57.6 us (98%)
  between operations  0.8 us (1%)
    pallas_call x1, Pallas kernels, local(): pl.pallas_call(functools.partial(step_kernel, (f0, f1, f2, w, d, h), back...  55 us
    pallas_call x1, Pallas kernels, local(): pl.pallas_call(functools.partial(unpack_kernel, (f0, f1, f2, h, scales),...  2.58 us

profile of v5, /device:TPU:0, one launch (start us, length us, event | category | flops | bytes accessed | tf_op | source)
XLA Modules:
  0.0 58.4 jit_solution(9758578734354632991)
XLA Ops:
  0.6 55.0 %unet_step.1 = (bf16[512,128]{1,0:T(8,128)(2,1)S(1)}, f32[128,128]{1,0:T(8,128)S(1)}, bf16[1024,128]{1,0:T(8,128)(2,1)S(1)}, bf16[768,128]{1,0:T(8,128)(2,1)S(1)...) custom-call(bf16[512,128]{1,0:T(8,128)(2,1)} %bitcast.27, ...), custom_call_target="tpu_custom_call" | custom-call | tf_op jit(solution)/shard_map/unet_step/pallas_call | solution.py:897
  55.7 2.6 %unpack.1 = (bf16[512,128]{1,0:T(8,128)(2,1)}, f32[864,32]{1,0:T(8,128)}, f32[864,64]{1,0:T(8,128)}, f32[1728,128]{1,0:T(8,128)}, f32[27,64,192]{2,1,0:T(8,128)}...) custom-call(bf16[512,128]{1,0:T(8,128)(2,1)S(1)} %get-tuple-element.25.refs_0_, f32[128,128]{1,0:T(8,128)S(1)} %get-tuple-element.26.refs_1_, ...), custom_call_target="tpu_custom_call" | custom-call | tf_op jit(solution)/shard_map/unpack/pallas_call | solution.py:925

commit v6 on v5

--- a/solution.py
+++ b/solution.py
@@ -728,11 +728,11 @@
 
     conv(stacks.mg, ref.b_mid, spans[1], half_store, back=True)
     ref.outs.half[...] = ref.half_wide[...]
-    sums.low.step()
     sums.bota.step()
     sums.upb.step()
     wide_wgrad(sums.stem, beside(spans[0], lambda a, b: ref.stem_grad[a, b]), stacks.feat, spans[0])
     sums.stem.step()
+    sums.low.step()
     sums.botb.step()
     sums.upa.step()
 

time: 58.6 us -> 58.7 us (level)
  no operation moved by 1% of the time
where the time goes in v6:
time: 58.7 us; the launch traced here: 58.6 us
  Pallas kernels  57.8 us (98%)
  between operations  0.8 us (1%)
    pallas_call x1, Pallas kernels, local(): pl.pallas_call(functools.partial(step_kernel, (f0, f1, f2, w, d, h), back...  55.2 us
    pallas_call x1, Pallas kernels, local(): pl.pallas_call(functools.partial(unpack_kernel, (f0, f1, f2, h, scales),...  2.58 us

profile of v6, /device:TPU:0, one launch (start us, length us, event | category | flops | bytes accessed | tf_op | source)
XLA Modules:
  0.0 58.6 jit_solution(8222563675171367363)
XLA Ops:
  0.6 55.2 %unet_step.1 = (bf16[512,128]{1,0:T(8,128)(2,1)S(1)}, f32[128,128]{1,0:T(8,128)S(1)}, bf16[1024,128]{1,0:T(8,128)(2,1)S(1)}, bf16[768,128]{1,0:T(8,128)(2,1)S(1)...) custom-call(bf16[512,128]{1,0:T(8,128)(2,1)} %bitcast.27, ...), custom_call_target="tpu_custom_call" | custom-call | tf_op jit(solution)/shard_map/unet_step/pallas_call | solution.py:897
  55.8 2.6 %unpack.1 = (bf16[512,128]{1,0:T(8,128)(2,1)}, f32[864,32]{1,0:T(8,128)}, f32[864,64]{1,0:T(8,128)}, f32[1728,128]{1,0:T(8,128)}, f32[27,64,192]{2,1,0:T(8,128)}...) custom-call(bf16[512,128]{1,0:T(8,128)(2,1)S(1)} %get-tuple-element.25.refs_0_, f32[128,128]{1,0:T(8,128)S(1)} %get-tuple-element.26.refs_1_, ...), custom_call_target="tpu_custom_call" | custom-call | tf_op jit(solution)/shard_map/unpack/pallas_call | solution.py:925
